TPU v7x, 32 devices: a whole 2x2x4 slice. The times are simulated.
32 devices in a mesh: dp: 8 (over z, x), tensor: 4 (over y, core).
Axes of the slice: x: 2, y: 2, z: 4, core: 2. Of those that a mesh axis runs over, the one named last changes fastest.
Arguments:
- tokens: bfloat16 [16384, 768], P(('dp', 'tensor')), may hold values from -6 to 6
- cotangent: bfloat16 [16384, 768], P(('dp', 'tensor')), may hold values from -6 to 6
- seq_lengths: int32 [8, 2], P('dp'), may hold values from 256 to 1792, as said below
- w_query: bfloat16 [768, 768], P('dp', 'tensor'), may hold values from -0.21875 to 0.21875
- w_keyvalue: bfloat16 [768, 128], P('dp'), may hold values from -0.21875 to 0.21875
- w_out: bfloat16 [768, 768], P('dp', 'tensor'), may hold values from -3.5 to 3.5
- w_up: bfloat16 [768, 3072], P('dp', 'tensor'), may hold values from -0.21875 to 0.21875
- w_down: bfloat16 [768, 3072], P('dp', 'tensor'), may hold values from -0.109375 to 0.109375
- norm1_gain: bfloat16 [768], P('dp'), may hold values from 0.5 to 1.5
- norm1_bias: bfloat16 [768], P('dp'), may hold values from -3 to 3
- norm2_gain: bfloat16 [768], P('dp'), may hold values from 0.5 to 1.5
- norm2_bias: bfloat16 [768], P('dp'), may hold values from -3 to 3
Outputs:
- out_tokens: bfloat16 [16384, 768], P(('dp', 'tensor'))
- d_tokens: float32 [16384, 768], P(('dp', 'tensor'))
- d_query: float32 [768, 768], P('dp', 'tensor')
- d_keyvalue: float32 [768, 128], P('dp')
- d_out_weight: float32 [768, 768], P('dp', 'tensor')
- d_up: float32 [768, 3072], P('dp', 'tensor')
- d_down: float32 [768, 3072], P('dp', 'tensor')
- d_norm1_gain: float32 [768], P('dp')
- d_norm1_bias: float32 [768], P('dp')
- d_norm2_gain: float32 [768], P('dp')
- d_norm2_bias: float32 [768], P('dp')
Inputs may be any that keep to these rules, and one draw needn't show every extreme that they name: `seq_lengths`: each row holds the length of its pack's one sequence, from 1024 to 1792, then the padding after it; a row sums to 2048, and in some row the sequence is exactly 1792 long.
All inputs are finite; a program needn't handle non-finite values.
Results may differ from a plain program's by a relative error of at most 0.011.
Values may be sent and summed in bfloat16 or wider, within the bound.
A program may use at most 256 MiB of HBM per device.

v0:
```python
import functools
import math
import types

import jax
import jax.numpy as jnp
from jax import lax
from jax.experimental import pallas as pl
from jax.experimental.pallas import tpu as pltpu
from jax.sharding import PartitionSpec as P

ROT = 16
SEQ_LEAST = 1024
SEQ_MOST = 1792
BLOCK = 256
EPS = 1e-05
NEG = -1e30
F32 = jnp.float32
BF16 = jnp.bfloat16


def dot(left, right):
    return jnp.dot(left, right, preferred_element_type=F32)


def dot_rows(left, right):
    return lax.dot_general(left, right, (((0,), (0,)), ((), ())), preferred_element_type=F32)


def dot_cols(left, right):
    return lax.dot_general(left, right, (((1,), (1,)), ((), ())), preferred_element_type=F32)


def lanes_of(rows):
    return lax.broadcasted_iota(jnp.int32, (rows, 128), 1)


def swap_halves(x, lane):
    return jnp.where(lane < ROT // 2, pltpu.roll(x, 128 - ROT // 2, 1), pltpu.roll(x, ROT // 2, 1))


def three_parts(x):
    high = x.astype(BF16).astype(F32)
    middle = (x - high).astype(BF16).astype(F32)
    return high, middle, x - high - middle


def unit_heads(wide, heads):
    pieces = []
    for h in range(heads):
        piece = wide[:, h // 2 * 128 : h // 2 * 128 + 128]
        pieces.append(piece if h % 2 == 0 else pltpu.roll(piece, 64, 1))
    return pieces


def join_heads(pieces, lane):
    wide = []
    for h in range(0, len(pieces), 2):
        second = pltpu.roll(pieces[h + 1], 64, 1) if h + 1 < len(pieces) else jnp.zeros_like(pieces[h])
        wide.append(jnp.where(lane < 64, pieces[h], second))
    return jnp.concatenate(wide, axis=1)


class Core:
    def __init__(self, heads, length, **refs):
        self.heads, self.length = heads, length
        self.__dict__.update(refs)
        stack, used = heads * BLOCK, self.d_query.shape[0]
        self.d_stack = self.scores.at[0:stack, 0:128]
        self.d_keys = self.scores.at[stack : stack + used, 0:128]
        self.d_values = self.scores.at[stack : stack + used, 128:256]

    def past(self, first, shape, axis):
        return lax.broadcasted_iota(jnp.int32, shape, axis) + first >= self.length

    def tables(self, part):
        count = self.cosine.shape[0] // BLOCK // 2

        @pl.loop(part * count, part * count + count)
        def _(index):
            at = pl.ds(pl.multiple_of(index * BLOCK, BLOCK), BLOCK)
            lane = lanes_of(BLOCK)
            row = lax.broadcasted_iota(jnp.int32, (BLOCK, 128), 0) + index * BLOCK
            position = jnp.where(row >= self.length, row - self.length, row).astype(F32)
            exponent = jnp.where(lane < ROT // 2, lane, lane - ROT // 2).astype(F32) * (-2.0 / ROT)
            angle = position * jnp.exp(exponent * math.log(10000.0))
            sine = jnp.sin(angle)
            self.cosine[at] = jnp.where(lane < ROT, jnp.cos(angle), 1.0)
            self.sine[at] = jnp.where(lane < ROT // 2, -sine, jnp.where(lane < ROT, sine, 0.0))

    def unpack_params(self):
        start = self.heads * 64
        turned = self.w_query[:, start // 128 * 128 : start // 128 * 128 + 128].T.astype(F32)
        self.params[0:4] = turned[start % 128 : start % 128 + 4]

    def normalize(self, block):
        at = pl.ds(pl.multiple_of(block * BLOCK, BLOCK), BLOCK)
        x = self.tokens[at].astype(F32)
        centered = x - jnp.mean(x, axis=1, keepdims=True)
        scaled = centered * lax.rsqrt(jnp.mean(centered * centered, axis=1, keepdims=True) + EPS)
        gain1, bias1, gain2, bias2 = (self.params[i : i + 1] for i in range(4))
        self.scaled[at] = scaled.astype(BF16)
        self.normed1[at] = (scaled * gain1 + bias1).astype(BF16)
        self.normed2[at] = (scaled * gain2 + bias2).astype(BF16)

    def project(self, block):
        first = pl.multiple_of(block * BLOCK, BLOCK)
        at = pl.ds(first, BLOCK)
        lane = lanes_of(BLOCK)
        cosine, sine = self.cosine[at], self.sine[at]
        past = self.past(first, (BLOCK, 128), 0)
        normed = self.normed1[at]
        key_value = dot(normed, self.w_keyvalue[...])
        keys = key_value * cosine + swap_halves(key_value, lane) * sine
        hidden_key = jnp.where(past, 0.0, NEG)
        extra = jnp.where(lane == 64, hidden_key, jnp.where(lane < 68, -1.0, 0.0))
        self.keys[at] = jnp.where(lane < 64, keys, extra).astype(BF16)
        ones = jnp.where(lane < 67, 1.0, 0.0)
        self.values[at] = jnp.where(lane < 64, pltpu.roll(key_value, 64, 1), ones).astype(BF16)
        query = dot(normed, self.w_query[...])
        flag = jnp.where((lane == 64) & past, 1.0, 0.0)
        for h, piece in enumerate(unit_heads(query, self.heads)):
            turned = (piece * cosine + swap_halves(piece, lane) * sine).astype(BF16).astype(F32)
            turned = turned * (64 ** (-0.5))
            self.queries[block, h * BLOCK : (h + 1) * BLOCK] = jnp.where(lane < 64, turned, flag).astype(BF16)

    def key_blocks(self, block):
        first = SEQ_LEAST // BLOCK if block * BLOCK >= SEQ_MOST else 0
        return range(first, block + 1)

    def attend(self, block):
        rows = self.heads * BLOCK
        query = self.queries[block]
        lane = lanes_of(rows)
        top = jnp.full((rows, BLOCK), -3e38, F32)
        for index, j in enumerate(self.key_blocks(block)):
            scores = dot_cols(query, self.keys[j * BLOCK : (j + 1) * BLOCK])
            if j == block:
                row = lax.rem(lax.broadcasted_iota(jnp.int32, (rows, BLOCK), 0), BLOCK)
                column = lax.broadcasted_iota(jnp.int32, (rows, BLOCK), 1)
                scores = jnp.where(column <= row, scores, NEG)
            self.scores[index * rows : (index + 1) * rows] = scores
            top = jnp.maximum(top, scores)
        top = jnp.max(top, axis=1, keepdims=True)
        total = jnp.zeros((rows, 128), F32)
        for index, j in enumerate(self.key_blocks(block)):
            probs = jnp.exp(self.scores[index * rows : (index + 1) * rows] - top).astype(BF16)
            total = total + dot(probs, self.values[j * BLOCK : (j + 1) * BLOCK])
        weight = jnp.sum(jnp.where(lane == 64, total, 0.0), axis=1, keepdims=True)
        output = total / weight
        pieces = [output[h * BLOCK : (h + 1) * BLOCK] for h in range(self.heads)]
        self.attended[block * BLOCK : (block + 1) * BLOCK] = join_heads(pieces, lanes_of(BLOCK)).astype(BF16)
        high, middle, low = three_parts(top + jnp.log(weight))
        parts = jnp.where(lane == 65, high, jnp.where(lane == 66, middle, low))
        self.queries[block] = jnp.where((lane >= 65) & (lane < 68), parts, query.astype(F32)).astype(BF16)

    def feed(self, at):
        up = dot(self.normed2[at], self.w_up[...])
        normal = 0.5 * (1.0 + lax.erf(up * (1.0 / math.sqrt(2.0))))
        self.hidden[at] = (up * normal).astype(BF16)
        density = jnp.exp(-0.5 * up * up) * (1.0 / math.sqrt(2.0 * math.pi))
        self.slope[at] = (normal + up * density).astype(BF16)

    def mix(self, at):
        return dot_cols(self.attended[at], self.w_out[...]) + dot_cols(self.hidden[at], self.w_down[...])

    def mask(self, at, first, rows):
        past = self.past(first, (rows, 1), 0)
        self.grad[at] = jnp.where(past, 0.0, self.cotangent[at].astype(F32)).astype(BF16)

    def feed_back(self, at):
        d_hidden = dot(self.grad[at], self.w_down[...])
        self.slope[at] = (d_hidden * self.slope[at].astype(F32)).astype(BF16)

    def attend_grad(self, block):
        first = pl.multiple_of(block * BLOCK, BLOCK)
        at = pl.ds(first, BLOCK)
        lane = lanes_of(BLOCK)
        grads = unit_heads(dot(self.grad[at], self.w_out[...]), self.heads)
        outputs = unit_heads(self.attended[at].astype(F32), self.heads)
        for h in range(self.heads):
            grad = grads[h].astype(BF16).astype(F32)
            delta = jnp.sum(jnp.where(lane < 64, grad * outputs[h], 0.0), axis=1, keepdims=True)
            high, middle, low = three_parts(-delta)
            parts = jnp.where(lane == 64, high, jnp.where(lane == 65, middle, jnp.where(lane == 66, low, 0.0)))
            self.d_attended[block, h * BLOCK : (h + 1) * BLOCK] = jnp.where(lane < 64, grad, parts).astype(BF16)

    def attend_back(self, block):
        rows = self.heads * BLOCK
        query, grad = self.queries[block], self.d_attended[block]

        def span(first, size, diagonal):
            at = pl.ds(pl.multiple_of(first, BLOCK), size)
            keys, values = self.keys[at], self.values[at]
            scores, d_probs = dot_cols(keys, query), dot_cols(values, grad)
            if diagonal:
                key = lax.broadcasted_iota(jnp.int32, (size, rows), 0)
                row = lax.rem(lax.broadcasted_iota(jnp.int32, (size, rows), 1), BLOCK) + (size - BLOCK)
                scores = jnp.where(key <= row, scores, NEG)
            probs = jnp.exp(scores)
            d_scores = (probs * d_probs).astype(BF16)
            self.d_values[at] += dot(probs.astype(BF16), grad)
            self.d_keys[at] += dot(d_scores, query)
            d_query = dot_rows(d_scores, keys)
            if diagonal:
                self.d_stack[...] = d_query
            else:
                self.d_stack[...] += d_query

        @pl.when(block % 2 == 1)
        def _():
            span((block - 1) * BLOCK, 2 * BLOCK, True)

        @pl.when(block % 2 == 0)
        def _():
            span(block * BLOCK, BLOCK, True)

        @pl.loop(0, block // 2)
        def _(index):
            span(index * 2 * BLOCK, 2 * BLOCK, False)

        at = pl.ds(pl.multiple_of(block * BLOCK, BLOCK), BLOCK)
        lane = lanes_of(BLOCK)
        cosine, sine = self.cosine[at], self.sine[at]

        def turn_back(x):
            return x * cosine - swap_halves(x, lane) * sine

        pieces = [
            turn_back(self.d_stack[h * BLOCK : (h + 1) * BLOCK]) * (64 ** (-0.5)) for h in range(self.heads)
        ]
        self.d_query[at] = join_heads(pieces, lane).astype(BF16)
        self.d_keyvalue[at] = jnp.where(
            lane < 64, turn_back(self.d_keys[at]), pltpu.roll(self.d_values[at], 64, 1)
        ).astype(BF16)

    def input_grad(self, block):
        at = pl.ds(pl.multiple_of(block * BLOCK, BLOCK), BLOCK)
        d_normed1 = dot_cols(self.d_query[at], self.w_query[...]) + dot_cols(self.d_keyvalue[at], self.w_keyvalue[...])
        d_normed2 = dot_cols(self.slope[at], self.w_up[...])
        scaled = self.scaled[at].astype(F32)
        for i, value in enumerate((d_normed1 * scaled, d_normed1, d_normed2 * scaled, d_normed2)):
            self.d_norms[i] += jnp.sum(value.reshape(BLOCK // 8, 8, -1), axis=0)
        return d_normed1 * self.params[0:1] + d_normed2 * self.params[2:3]


MESH = pl.DeviceIdType.MESH
INVMEM = pl.BlockSpec(memory_space=pltpu.VMEM)


class Axis:
    def __init__(self, name, size):
        self.name, self.size, self.half = name, size, size // 2
        self.me = lax.axis_index(name)
        self.row, self.par = self.me // 2, self.me % 2
        self.pair = self.me + 1 - 2 * self.par

    def other_row(self, step):
        return lax.rem(self.row + step + self.half, self.half)

    def line(self, step):
        return self.other_row(step) * 2 + self.par

    def greet(self, barrier):
        for step in range(1, self.size):
            peer = lax.rem(self.me + step, self.size)
            pl.semaphore_signal(barrier, inc=1, device_id={self.name: peer}, device_id_type=MESH)
        return self.size - 1


def remote(src, dst, send, recv, axis, peer):
    return pltpu.make_async_remote_copy(
        src_ref=src, dst_ref=dst, send_sem=send, recv_sem=recv, device_id={axis.name: peer}, device_id_type=MESH
    )


def part_of(ref, index, rows):
    return ref.at[pl.ds(pl.multiple_of(index * rows, rows), rows)]


class Gather:
    def __init__(self, axis, src, dst, send, recv, local):
        self.axis, self.src, self.dst, self.send, self.recv = axis, src, dst, send, recv
        self.half = axis.half
        self.copy = pltpu.make_async_copy(src, self.slot(axis.me), local)

    def slot(self, index):
        return part_of(self.dst, index, self.src.shape[0])

    def along(self, row, way, own=False):
        slot = self.slot(2 * row + self.axis.par)
        send = self.send.at[row if way > 0 else self.half + row]
        peer = self.axis.me + 2 * way
        return remote(self.src if own else slot, slot, send, self.recv.at[row], self.axis, peer)

    def across(self, row, own=False):
        slot = self.slot(2 * row + self.axis.par)
        sems = self.send.at[2 * self.half + row], self.recv.at[self.half + row]
        return remote(self.src if own else slot, slot, *sems, self.axis, self.axis.pair)

    def start_line(self):
        @pl.when(self.axis.row + 1 < self.half)
        def _():
            self.along(self.axis.row, 1, own=True).start()

        @pl.when(self.axis.row > 0)
        def _():
            self.along(self.axis.row, -1, own=True).start()

    def start_pair(self):
        self.across(self.axis.row, own=True).start()

    def pass_on(self, distance):
        if distance >= self.half:
            return
        me = self.axis.row

        @pl.when(me >= distance)
        def _():
            row = me - distance
            self.along(row, 1).wait_recv()

            @pl.when(me + 1 < self.half)
            def _():
                self.along(row, 1).start()

            self.across(row).start()

        @pl.when(me + distance < self.half)
        def _():
            row = me + distance
            self.along(row, -1).wait_recv()

            @pl.when(me > 0)
            def _():
                self.along(row, -1).start()

            self.across(row).start()

    def pair_arrived(self, row):
        slot = self.slot(2 * row + 1 - self.axis.par)
        sems = self.send.at[2 * self.half + row], self.recv.at[self.half + row]
        remote(slot, slot, *sems, self.axis, self.axis.pair).wait_recv()

    def arrive(self):
        self.copy.wait()
        for row in range(self.half):
            self.pair_arrived(row)

    def leave(self):
        for row in range(self.half):
            self.across(row).wait_send()

            @pl.when((self.axis.row >= row) & (self.axis.row + 1 < self.half))
            def _():
                self.along(row, 1).wait_send()

            @pl.when((self.axis.row <= row) & (self.axis.row > 0))
            def _():
                self.along(row, -1).wait_send()


class Reduce:
    def __init__(self, axis, part, out, held, last, send, recv):
        self.axis, self.part, self.out, self.held, self.last = axis, part, out, held, last
        self.send, self.recv, self.rows = send, recv, out.shape[0]
        self.chunk = 32 if self.rows % 32 == 0 else self.rows

    def first(self, row):
        block = part_of(self.part, 2 * row + 1 - self.axis.par, self.rows)
        held = part_of(self.held, row, self.rows)
        return remote(block, held, self.send.at[row], self.recv.at[row], self.axis, self.axis.pair)

    def second(self, step):
        index = self.axis.half + step
        block = part_of(self.held, self.axis.other_row(step), self.rows)
        last = part_of(self.last, step - 1, self.rows)
        return remote(block, last, self.send.at[index], self.recv.at[index], self.axis, self.axis.line(step))

    def start(self):
        for step in range(self.axis.half):
            self.first(self.axis.other_row(step + 1)).start()

    def chunks(self, body):
        @pl.loop(0, self.rows // self.chunk)
        def _(index):
            body(pl.multiple_of(index * self.chunk, self.chunk))

    def total(self, row, at):
        part = self.part[pl.ds((2 * row + self.axis.par) * self.rows + at, self.chunk)].astype(F32)
        return part + self.held[pl.ds(row * self.rows + at, self.chunk)].astype(F32)

    def middle(self):
        for step in range(1, self.axis.half):
            row = self.axis.other_row(step)
            self.first(row).wait()

            def add(at, row=row):
                self.held[pl.ds(row * self.rows + at, self.chunk)] = self.total(row, at).astype(self.held.dtype)

            self.chunks(add)
            self.second(step).start()

        self.first(self.axis.row).wait()

        def keep(at):
            self.out[pl.ds(at, self.chunk)] = self.total(self.axis.row, at)

        self.chunks(keep)

    def end(self):
        for step in range(1, self.axis.half):
            self.second(step).wait()

        def add(at):
            total = self.out[pl.ds(at, self.chunk)]
            for step in range(1, self.axis.half):
                total = total + self.last[pl.ds((step - 1) * self.rows + at, self.chunk)].astype(F32)
            self.out[pl.ds(at, self.chunk)] = total

        self.chunks(add)


class Stream:
    def __init__(self, axis, part, out, held, last, pair_send, pair_recv, line_send, line_recv):
        self.axis, self.part, self.out, self.held, self.last = axis, part, out, held, last
        self.pair_sems, self.line_sems = (pair_send, pair_recv), (line_send, line_recv)

    def split(self, chunk):
        return chunk // 4, chunk // 2 % 2, chunk % 2

    def pair_copy(self, chunk):
        row, _, half = self.split(chunk)
        index = 2 * row + half
        send, recv = (sems.at[index] for sems in self.pair_sems)
        held = part_of(self.held, index, BLOCK)
        return remote(part_of(self.part, chunk, BLOCK), held, send, recv, self.axis, self.axis.pair)

    def line_copy(self, chunk):
        row, _, half = self.split(chunk)
        send, recv = (sems.at[half] for sems in self.line_sems)
        held = part_of(self.held, 2 * row + half, BLOCK)
        return remote(held, part_of(self.last, half, BLOCK), send, recv, self.axis, self.axis.line(1))

    def give(self, chunk):
        @pl.when(self.axis.par != self.split(chunk)[1])
        def _():
            self.pair_copy(chunk).start()

    def take(self, chunk):
        row, par, half = self.split(chunk)

        @pl.when(self.axis.par == par)
        def _():
            self.pair_copy(chunk).wait_recv()

            def total(at):
                part = self.part[pl.ds(chunk * BLOCK + at, 32)].astype(F32)
                return part + self.held[pl.ds((2 * row + half) * BLOCK + at, 32)].astype(F32)

            @pl.when(self.axis.row == row)
            def _():
                @pl.loop(0, BLOCK // 32)
                def _(index):
                    at = pl.multiple_of(index * 32, 32)
                    self.out[pl.ds(half * BLOCK + at, 32)] = total(at)

            @pl.when(self.axis.row != row)
            def _():
                @pl.loop(0, BLOCK // 32)
                def _(index):
                    at = pl.multiple_of(index * 32, 32)
                    self.held[pl.ds((2 * row + half) * BLOCK + at, 32)] = total(at).astype(BF16)

                self.line_copy(chunk).start()

    def end(self, chunk):
        row, par, half = self.split(chunk)

        @pl.when(self.axis.par != par)
        def _():
            self.pair_copy(chunk).wait_send()

        @pl.when((self.axis.par == par) & (self.axis.row != row))
        def _():
            self.line_copy(chunk).wait_send()

        @pl.when((self.axis.par == par) & (self.axis.row == row))
        def _():
            self.line_copy(chunk).wait_recv()

            @pl.loop(0, BLOCK // 32)
            def _(index):
                at = pl.multiple_of(index * 32, 32)
                rows = pl.ds(half * BLOCK + at, 32)
                self.out[rows] += self.last[rows].astype(F32)

WEIGHTS = ("w_query", "w_keyvalue", "w_up", "w_down", "w_out")
INPUTS = ("tokens", "cotangent") + WEIGHTS


def own_shapes(z):
    wide_rows = (z.rows, z.model)
    return dict(
        params=((8, z.model), F32), cosine=((z.rows, 128), F32), sine=((z.rows, 128), F32),
        normed1=(wide_rows, BF16), normed2=(wide_rows, BF16),
        queries=((z.rows // BLOCK, z.stack, 128), BF16), keys=((z.rows, 128), BF16), values=((z.rows, 128), BF16),
        scores=((z.used // BLOCK * z.stack, BLOCK), F32), attended=((z.rows, z.wide), BF16), hidden=((z.rows, z.units), BF16),
        slope=((z.rows, z.units), BF16), d_attended=((z.used // BLOCK, z.stack, 128), BF16),
        d_query=((z.used, z.wide), BF16), d_keyvalue=((z.used, 128), BF16), d_norms=((4, 8, z.model), F32),
    )


class Names:
    def __init__(self, names, refs):
        self.__dict__.update(zip(names, refs, strict=True))


def fused_specs(z):
    half, model = z.nd // 2, z.model
    columns = dict(zip(WEIGHTS, (z.wide, 128, z.units, z.units, z.wide)))
    arrays = own_shapes(z)
    arrays.update(pack_query=((z.own, z.wide), BF16), pack_out=((z.own, z.wide), BF16))
    arrays.update(tokens=((z.rows, model), BF16), cotangent=((z.rows, model), BF16))
    arrays.update({name: ((model, columns[name]), BF16) for name in WEIGHTS})
    arrays.update(mixed=((z.rows, model), BF16), held_mixed=((z.rows // 2, model), BF16))
    arrays.update(last_mixed=((z.slots, model), BF16), held_scaled=((z.rows // 2, model), BF16))
    arrays.update(last_scaled=((z.slots, model), BF16))
    for name in WEIGHTS:
        arrays["g_" + name] = ((model, columns[name]), BF16)
        arrays["held_" + name] = ((half * z.own, columns[name]), BF16)
        arrays["last_" + name] = ((max(half - 1, 1) * z.own, columns[name]), BF16)
    arrays.update(g_norms=((z.nd * 8, z.own), F32), held_norms=((half * 8, z.own), F32))
    arrays.update(last_norms=((max(half - 1, 1) * 8, z.own), F32))
    semaphores = dict(send_mixed=z.nt, recv_mixed=z.nt, send_norms=z.nd, recv_norms=z.nd)
    for name in INPUTS:
        count = z.nd if name in WEIGHTS else z.nt
        semaphores.update({"send_" + name: count // 2 * 3, "recv_" + name: count})
    for name in WEIGHTS:
        semaphores.update({"out_" + name: z.nd, "in_" + name: z.nd})
    semaphores.update(pair_send=4, pair_recv=4, line_send=2, line_recv=2, local=len(INPUTS))
    semaphores.update(share_send=2 * z.nt, share_recv=2 * z.nt)
    return arrays, semaphores


OUTPUTS = ("mixed_sum", "scaled_sum", "s_w_query", "s_w_out", "s_w_up", "s_w_down", "shared_kv", "shared_norms")


def fused_kernel(z, names, *refs):
    it = Names(("seq", "norms") + tuple("i_" + n for n in INPUTS) + OUTPUTS + names, refs)
    dp, tensor = Axis("dp", z.nd), Axis("tensor", z.nt)
    rows, model, used, slots = z.rows, z.model, z.used, z.slots
    core = Core(z.heads, it.seq[0, 0], **{n: getattr(it, n) for n in tuple(own_shapes(z)) + INPUTS}, grad=it.cotangent, scaled=it.tokens)
    barrier = pltpu.get_barrier_semaphore()
    expected = dp.greet(barrier) + tensor.greet(barrier)

    width = z.heads * 64
    pad = jnp.zeros((z.own, z.wide - width), BF16)
    lane = lanes_of(z.own)
    first = width // 128 * 128
    tail = jnp.concatenate([it.i_w_query[:, first:].astype(F32), pad.astype(F32)], axis=1)
    it.pack_query[:, :first] = it.i_w_query[:, :first]
    it.pack_query[:, first:] = jnp.where(lane < width - first, tail, it.norms[...].astype(F32)).astype(BF16)
    it.pack_out[:, :first] = it.i_w_out[:, :first]
    it.pack_out[:, first:] = jnp.concatenate([it.i_w_out[:, first:], pad], axis=1)
    sources = dict(w_query=it.pack_query, w_out=it.pack_out)
    g = {}
    for i, name in enumerate(INPUTS):
        axis = tensor if name in ("tokens", "cotangent") else dp
        source = sources.get(name, getattr(it, "i_" + name))
        sems = getattr(it, "send_" + name), getattr(it, "recv_" + name)
        g[name] = Gather(axis, source, getattr(it, name), *sems, it.local.at[i])
    pl.semaphore_wait(barrier, expected)

    def hand_on(names, distance):
        for name in names:
            g[name].pass_on(distance)

    small = ("w_query", "w_keyvalue")
    for name in ("tokens", "cotangent"):
        g[name].start_line()
        g[name].start_pair()
    for name in small:
        g[name].start_line()
        g[name].start_pair()
    g["w_up"].start_pair()
    for name in INPUTS:
        g[name].copy.start()
    core.tables(0)
    hand_on(small, 1)
    g["w_up"].start_line()
    core.tables(1)
    hand_on(small, 2)
    g["w_down"].start_pair()
    hand_on(small, 3)
    hand_on(("w_up",), 1)
    g["w_down"].start_line()
    for name in small:
        g[name].arrive()
    core.unpack_params()

    def enter(slot):
        for part in range(slots // BLOCK):
            core.normalize(slot * (slots // BLOCK) + part)
            core.project(slot * (slots // BLOCK) + part)

    g["tokens"].copy.wait()

    @pl.loop(0, 4)
    def _(index):
        @pl.when(index == 1)
        def _():
            g["tokens"].pair_arrived(tensor.row)
            hand_on(("w_up",), 2)
            g["w_out"].start_pair()

        @pl.when(index == 2)
        def _():
            hand_on(("w_up",), 3)
            hand_on(("w_down",), 1)
            g["w_out"].start_line()
            g["tokens"].pass_on(1)
            g["tokens"].leave()

        @pl.when(index == 3)
        def _():
            g["tokens"].pair_arrived(1 - tensor.row)
            hand_on(("w_down",), 2)

        enter(tensor.me + lax.rem(index, 2) * (tensor.pair - tensor.me) + index // 2 * (tensor.line(1) - tensor.me))

    for block in range(rows // BLOCK):
        core.attend(block)
        if block == 3:
            hand_on(("w_down",), 3)
            hand_on(("w_out",), 1)
        if block == 5:
            hand_on(("w_out",), 2)
    hand_on(("w_out",), 3)
    g["w_up"].arrive()

    @pl.loop(0, rows // slots)
    def _(index):
        core.feed(pl.ds(pl.multiple_of(index * slots, slots), slots))

    g["cotangent"].pass_on(1)
    g["w_down"].arrive()
    g["cotangent"].arrive()
    g["cotangent"].leave()

    quarter = used // 4

    @pl.loop(0, 4)
    def _(index):
        first = pl.multiple_of(index * quarter, quarter)
        core.mask(pl.ds(first, quarter), first, quarter)

    r = {}
    for name in WEIGHTS:
        out = getattr(it, "s_" + name) if name != "w_keyvalue" else it.shared_kv.at[tensor.me]
        some = [getattr(it, kind + name) for kind in ("g_", "held_", "last_", "out_", "in_")]
        r[name] = Reduce(dp, some[0], out, *some[1:])
    r["norms"] = Reduce(
        dp, it.g_norms, it.shared_norms.at[tensor.me], it.held_norms, it.last_norms, it.send_norms, it.recv_norms
    )
    r["mixed"] = Reduce(tensor, it.mixed, it.mixed_sum, it.held_mixed, it.last_mixed, it.send_mixed, it.recv_mixed)
    scaled = Stream(
        tensor, it.mixed, it.scaled_sum, it.held_scaled, it.last_scaled,
        it.pair_send, it.pair_recv, it.line_send, it.line_recv,
    )

    def weight_grad(name, left, right):
        @pl.loop(0, model // BLOCK)
        def _(index):
            at = pl.ds(pl.multiple_of(index * BLOCK, BLOCK), BLOCK)
            r[name].part[at] = dot_rows(left[:used, at], right[:used]).astype(BF16)

    weight_grad("w_down", core.grad, core.hidden)
    r["w_down"].start()
    weight_grad("w_out", core.grad, core.attended)
    r["w_out"].start()
    g["w_out"].arrive()

    @pl.loop(0, tensor.size)
    def _(index):
        row = lax.rem(index, tensor.half)
        par = jnp.where(index < tensor.half, 1 - tensor.par, tensor.par)
        at = pl.ds(pl.multiple_of((2 * row + par) * slots, slots), slots)
        it.mixed[at] = core.mix(at).astype(BF16)

        @pl.when(index < tensor.half)
        def _():
            r["mixed"].first(row).start()

    @pl.loop(0, 4)
    def _(index):
        core.feed_back(pl.ds(pl.multiple_of(index * quarter, quarter), quarter))

    weight_grad("w_up", core.normed2, core.slope)
    r["w_up"].start()
    r["mixed"].middle()

    @pl.loop(0, used // BLOCK)
    def _(block):
        core.attend_grad(block)

    r["w_down"].middle()
    for ref in (core.d_keys, core.d_values, core.d_norms, it.scaled_sum):
        ref[...] = jnp.zeros_like(ref)
    chunks = used // BLOCK

    @pl.loop(0, chunks)
    def _(index):
        block = chunks - 1 - index
        core.attend_back(block)
        part_of(it.mixed, block, BLOCK)[...] = core.input_grad(block).astype(BF16)
        scaled.give(block)

        @pl.when(index > 0)
        def _():
            scaled.take(block + 1)

        @pl.when(index == 1)
        def _():
            r["w_out"].middle()

        @pl.when(index == 3)
        def _():
            r["w_up"].middle()

    weight_grad("w_query", core.normed1, core.d_query)
    r["w_query"].start()
    weight_grad("w_keyvalue", core.normed1, core.d_keyvalue)
    r["w_keyvalue"].start()
    part = model // dp.size
    sums = jnp.concatenate([jnp.sum(core.d_norms[i], axis=0, keepdims=True) for i in range(4)] + [jnp.zeros((4, model), F32)])
    for i in range(dp.size):
        it.g_norms[i * 8 : (i + 1) * 8] = sums[:, i * part : (i + 1) * part]
    r["norms"].start()
    scaled.take(0)
    for name in ("w_query", "w_keyvalue", "norms"):
        r[name].middle()
    for name in ("w_keyvalue", "norms"):
        r[name].end()
    copies = []
    for i, ref in enumerate((it.shared_kv, it.shared_norms)):
        for step in range(1, tensor.size):
            peer = lax.rem(tensor.me + step, tensor.size)
            sems = [s.at[i * tensor.size + step] for s in (it.share_send, it.share_recv)]
            copies.append(remote(ref.at[tensor.me], ref.at[tensor.me], *sems, tensor, peer))
            copies[-1].start()
    for name in ("w_down", "w_out", "w_up", "mixed", "w_query"):
        r[name].end()
    @pl.loop(0, chunks)
    def _(index):
        scaled.end(chunks - 1 - index)

    for copy in copies:
        copy.wait()
    for name in INPUTS:
        if name in WEIGHTS:
            g[name].leave()


def finish_kernel(heads, seq, tokens, cotangent, *refs):
    sums = Names(OUTPUTS, refs[: len(OUTPUTS)])
    out_tokens, d_tokens, d_query, d_keyvalue, d_out, d_up, d_down, d_norms = refs[len(OUTPUTS) :]
    rows, chunk = tokens.shape[0], 128
    first_row = lax.axis_index("tensor") * rows

    @pl.loop(0, rows // chunk)
    def _(index):
        first = pl.multiple_of(index * chunk, chunk)
        at = pl.ds(first, chunk)
        token = tokens[at].astype(F32)
        out_tokens[at] = (token + sums.mixed_sum[at]).astype(BF16)
        centered = token - jnp.mean(token, axis=1, keepdims=True)
        inv_std = lax.rsqrt(jnp.mean(centered * centered, axis=1, keepdims=True) + EPS)
        scaled = centered * inv_std
        grad = sums.scaled_sum[at]
        row = lax.broadcasted_iota(jnp.int32, (chunk, 1), 0) + first + first_row
        own = jnp.where(row < seq[0, 0], cotangent[at].astype(F32), 0.0)
        inner = jnp.mean(grad * scaled, axis=1, keepdims=True)
        d_tokens[at] = own + inv_std * (grad - jnp.mean(grad, axis=1, keepdims=True) - scaled * inner)

    d_query[...] = sums.s_w_query[:, : heads * 64]
    d_out[...] = sums.s_w_out[:, : heads * 64]
    d_up[...] = sums.s_w_up[...]
    d_down[...] = sums.s_w_down[...]
    kv, norms = sums.shared_kv[0], sums.shared_norms[0]
    for t in range(1, sums.shared_kv.shape[0]):
        kv, norms = kv + sums.shared_kv[t], norms + sums.shared_norms[t]
    d_keyvalue[...] = kv
    d_norms[...] = norms


def plain_kernel(z, seq, *refs):
    named = dict(zip(INPUTS, refs))
    mixed, scaled_grad, g_query, g_keyvalue, g_out, g_up, g_down, g_norms = refs[len(INPUTS) : len(INPUTS) + 8]
    *own, grad, scaled = refs[len(INPUTS) + 8 :]
    named.update(zip(own_shapes(z), own), grad=grad, scaled=scaled)
    core = Core(z.heads, seq[0, 0], **named)
    rows, model, used = z.rows, z.model, z.used
    core.tables(0)
    core.tables(1)
    core.unpack_params()

    @pl.loop(0, rows // BLOCK)
    def _(block):
        core.normalize(block)
        core.project(block)

    for block in range(rows // BLOCK):
        core.attend(block)

    @pl.loop(0, rows // 512)
    def _(index):
        at = pl.ds(pl.multiple_of(index * 512, 512), 512)
        core.feed(at)
        mixed[at] = core.mix(at).astype(BF16)

    @pl.loop(0, 4)
    def _(index):
        first = pl.multiple_of(index * (used // 4), used // 4)
        core.mask(pl.ds(first, used // 4), first, used // 4)
        core.feed_back(pl.ds(first, used // 4))

    @pl.loop(0, used // BLOCK)
    def _(block):
        core.attend_grad(block)

    @pl.loop(0, model // BLOCK)
    def _(index):
        at = pl.ds(pl.multiple_of(index * BLOCK, BLOCK), BLOCK)
        grad = core.grad[:used, at]
        g_down[at] = dot_rows(grad, core.hidden[:used]).astype(BF16)
        g_out[at] = dot_rows(grad, core.attended[:used]).astype(BF16)
        g_up[at] = dot_rows(core.normed2[:used, at], core.slope[:used]).astype(BF16)

    for ref in (core.d_keys, core.d_values, core.d_norms):
        ref[...] = jnp.zeros_like(ref)
    @pl.loop(0, used // BLOCK)
    def _(index):
        block = used // BLOCK - 1 - index
        core.attend_back(block)
        part_of(scaled_grad, block, BLOCK)[...] = core.input_grad(block).astype(BF16)

    scaled_grad[used:] = jnp.zeros((rows - used, model), BF16)

    @pl.loop(0, model // BLOCK)
    def _(index):
        at = pl.ds(pl.multiple_of(index * BLOCK, BLOCK), BLOCK)
        normed = core.normed1[:used, at]
        g_query[at] = dot_rows(normed, core.d_query[:used]).astype(BF16)
        g_keyvalue[at] = dot_rows(normed, core.d_keyvalue[:used]).astype(BF16)

    for i in range(4):
        g_norms[i : i + 1] = jnp.sum(core.d_norms[i], axis=0, keepdims=True)


def run_plain(seq_lengths, norms, arrays, z):
    tokens, cotangent, w_query, w_keyvalue, w_up, w_down, w_out = arrays
    width, model = w_query.shape[1], tokens.shape[1]
    wide = z.wide
    pad = jnp.pad(w_query[:, width // 128 * 128 :], ((0, 0), (0, wide - width)))
    lane = lax.iota(jnp.int32, 128)[None]
    tail = jnp.where(lane < width % 128, pad, norms)
    query = jnp.concatenate([w_query[:, : width // 128 * 128], tail], axis=1)
    out = jnp.pad(w_out, ((0, 0), (0, wide - width)))
    gathered = [lax.all_gather(a, "tensor", axis=0, tiled=True) for a in (tokens, cotangent)]
    gathered += [lax.all_gather(a, "dp", axis=0, tiled=True) for a in (query, w_keyvalue, w_up, w_down, out)]
    shape = jax.ShapeDtypeStruct
    results = pl.pallas_call(
        functools.partial(plain_kernel, z),
        out_shape=[shape((z.rows, model), BF16)] * 2
        + [shape((model, n), BF16) for n in (wide, 128, wide, z.units, z.units)]
        + [shape((4, model), F32)],
        in_specs=[pl.BlockSpec(memory_space=pltpu.SMEM)] + [INVMEM] * len(gathered),
        out_specs=[INVMEM] * 8,
        scratch_shapes=[pltpu.VMEM(*entry) for entry in own_shapes(z).values()] + [pltpu.VMEM((n, model), BF16) for n in (z.used, z.rows)],
        compiler_params=pltpu.CompilerParams(vmem_limit_bytes=67043328),
        name="plain_layer",
    )(seq_lengths, *gathered)
    names = ("tensor", "tensor") + ("dp",) * 5
    sums = [
        lax.psum_scatter(p.astype(F32), n, scatter_dimension=0, tiled=True) for p, n in zip(results[:7], names)
    ]
    norm_sums = lax.psum_scatter(results[7], "dp", scatter_dimension=1, tiled=True)
    shared_kv = lax.all_gather(sums[3], "tensor")
    shared_norms = lax.all_gather(jnp.pad(norm_sums, ((0, 4), (0, 0))), "tensor")
    return sums[0], sums[1], sums[2], sums[4], sums[5], sums[6], shared_kv, shared_norms


def run_whole(seq_lengths, norms, arrays, z):
    arrays_of, semaphores = fused_specs(z)
    shapes = [
        (z.slots, z.model), (z.slots, z.model), (z.own, z.wide), (z.own, z.wide), (z.own, z.units), (z.own, z.units),
        (z.nt, z.own, 128), (z.nt, 8, z.own),
    ]
    scratch = [pltpu.VMEM(*entry) for entry in arrays_of.values()]
    scratch += [pltpu.SemaphoreType.DMA((count,)) for count in semaphores.values()]
    return pl.pallas_call(
        functools.partial(fused_kernel, z, tuple(arrays_of) + tuple(semaphores)),
        out_shape=[jax.ShapeDtypeStruct(shape, F32) for shape in shapes],
        in_specs=[pl.BlockSpec(memory_space=pltpu.SMEM)] + [INVMEM] * (1 + len(arrays)),
        out_specs=[INVMEM] * len(shapes),
        scratch_shapes=scratch,
        compiler_params=pltpu.CompilerParams(collective_id=0, has_side_effects=True, vmem_limit_bytes=67043328),
        name="layer",
    )(seq_lengths, norms, *arrays)


def run_layer(seq_lengths, norms, arrays, nd, nt):
    tokens, _, w_query, w_keyvalue, w_up, _, _ = arrays
    heads, own, units = w_query.shape[1] // 64, w_query.shape[0], w_up.shape[1]
    slots, model = tokens.shape
    z = types.SimpleNamespace(
        nd=nd, nt=nt, heads=heads, rows=slots * nt, model=model, stack=heads * BLOCK, units=units, used=SEQ_MOST,
        wide=(heads * 64 + 4 + 127) // 128 * 128, own=own, slots=slots,
    )
    run = run_whole if own % 32 == 0 and slots == 2 * BLOCK and nt == 4 else run_plain
    sums = run(seq_lengths, norms, arrays, z)
    shape = jax.ShapeDtypeStruct
    results = pl.pallas_call(
        functools.partial(finish_kernel, heads),
        out_shape=[
            shape((slots, model), BF16), shape((slots, model), F32), shape((own, heads * 64), F32), shape((own, 128), F32),
            shape((own, heads * 64), F32), shape((own, units), F32), shape((own, units), F32), shape((8, own), F32),
        ],
        in_specs=[pl.BlockSpec(memory_space=pltpu.SMEM)] + [INVMEM] * (2 + len(sums)),
        out_specs=[INVMEM] * 8,
        compiler_params=pltpu.CompilerParams(vmem_limit_bytes=67043328),
        name="finish",
    )(seq_lengths, *arrays[:2], *sums)
    return tuple(results[:7]) + tuple(results[7][i] for i in range(4))


def shards(
    tokens,
    cotangent,
    seq_lengths,
    w_query,
    w_keyvalue,
    w_out,
    w_up,
    w_down,
    norm1_gain,
    norm1_bias,
    norm2_gain,
    norm2_bias,
):
    start = w_query.shape[1] % 128
    norms = jnp.stack([norm1_gain, norm1_bias, norm2_gain, norm2_bias], axis=1)
    norms = jnp.pad(norms, ((0, 0), (start, 124 - start)))
    arrays = (tokens, cotangent, w_query, w_keyvalue, w_up, w_down, w_out)
    return run_layer(seq_lengths, norms, arrays, lax.axis_size("dp"), lax.axis_size("tensor"))


def solution(mesh):
    return jax.shard_map(
        shards,
        mesh=mesh,
        in_specs=(
            P(("dp", "tensor"), None),
            P(("dp", "tensor"), None),
            P("dp", None),
            P("dp", "tensor"),
            P("dp", None),
            P("dp", "tensor"),
            P("dp", "tensor"),
            P("dp", "tensor"),
            P("dp"),
            P("dp"),
            P("dp"),
            P("dp"),
        ),
        out_specs=(
            P(("dp", "tensor"), None),
            P(("dp", "tensor"), None),
            P("dp", "tensor"),
            P("dp", None),
            P("dp", "tensor"),
            P("dp", "tensor"),
            P("dp", "tensor"),
            P("dp"),
            P("dp"),
            P("dp"),
            P("dp"),
        ),
        check_vma=False,
    )
```

profile of v0, /device:TPU:0, one launch (start us, length us, event | category | flops | bytes accessed | tf_op | source)
XLA Modules:
  0.0 129.2 jit_solution(2567262945200682910)
XLA Ops:
  0.6 0.7 pad_maximum_fusion
  1.4 0.1 copy.27
  1.5 0.7 pad.4.refs_1_
  2.2 120.0 %layer.1 = (f32[512,768]{1,0:T(8,128)}, f32[512,768]{1,0:T(8,128)}, f32[96,256]{1,0:T(8,128)}, f32[96,256]{1,0:T(8,128)}, f32[96,768]{1,0:T(8,128)}, /*index=5*/...) custom-call(s32[1,2]{1,0:T(1,128)} %seq.1, bf16[96,128]{1,0:T(8,128)(2,1)} %pad.4.refs_1_, ...), custom_call_target="tpu_custom_call" | custom-call | tf_op jit(solution)/shard_map/layer/pallas_call | solution.py:902
  122.2 5.6 %finish.1 = (bf16[512,768]{1,0:T(8,128)(2,1)}, f32[512,768]{1,0:T(8,128)}, f32[96,192]{1,0:T(8,128)}, f32[96,128]{1,0:T(8,128)}, f32[96,192]{1,0:T(8,128)}, /*in...) custom-call(s32[1,2]{1,0:T(1,128)} %seq.1, bf16[512,768]{1,0:T(8,128)(2,1)} %tokens.1, ...), custom_call_target="tpu_custom_call" | custom-call | tf_op jit(solution)/shard_map/finish/pallas_call | solution.py:924
  127.8 1.4 %slice_bitcast_fusion = (f32[96]{0:T(128)}, f32[96]{0:T(128)}, f32[96]{0:T(128)}, f32[96]{0:T(128)}) fusion(f32[8,96]{1,0:T(8,128)} %get-tuple-element.42), kind=kLoop, calls=%fused_computation.1 | loop fusion | bytes 3072 | tf_op jit(solution)/shard_map/squeeze | solution.py:935
where the time goes:
time: 129 us
  Pallas kernels  126 us (98%)
  local copies, waits for them, and re-layouts  2.18 us (2%)
    pallas_call x1, Pallas kernels, run_whole(): pl.pallas_call(functools.partial(fused_kernel, z, tuple(arrays_of) + tupl...  120 us
    pallas_call x1, Pallas kernels, run_layer(): pl.pallas_call(functools.partial(finish_kernel, heads), out_shape=[shape(...  5.63 us

commit v1 on v0

--- a/solution.py
+++ b/solution.py
@@ -65,7 +65,8 @@
     def __init__(self, heads, length, **refs):
         self.heads, self.length = heads, length
         self.__dict__.update(refs)
-        stack, used = heads * BLOCK, self.d_query.shape[0]
+        stack, used = heads * BLOCK, self.d_keyvalue.shape[0]
+        self.d_query = self.attended
         self.d_stack = self.scores.at[0:stack, 0:128]
         self.d_keys = self.scores.at[stack : stack + used, 0:128]
         self.d_values = self.scores.at[stack : stack + used, 128:256]
@@ -246,6 +247,7 @@
 
 MESH = pl.DeviceIdType.MESH
 INVMEM = pl.BlockSpec(memory_space=pltpu.VMEM)
+ANY = pl.BlockSpec(memory_space=pl.ANY)
 
 
 class Axis:
@@ -279,13 +281,14 @@
 
 
 class Gather:
-    def __init__(self, axis, src, dst, send, recv, local):
-        self.axis, self.src, self.dst, self.send, self.recv = axis, src, dst, send, recv
-        self.half = axis.half
-        self.copy = pltpu.make_async_copy(src, self.slot(axis.me), local)
+    def __init__(self, axis, src, dst, send, recv, local, part=0, parts=1):
+        self.axis, self.dst, self.send, self.recv = axis, dst, send, recv
+        self.half, self.part, self.parts = axis.half, part, parts
+        self.src = part_of(src, part, src.shape[0] // parts)
+        self.copy = pltpu.make_async_copy(self.src, self.slot(axis.me), local)
 
     def slot(self, index):
-        return part_of(self.dst, index, self.src.shape[0])
+        return part_of(self.dst, index * self.parts + self.part, self.src.shape[0])
 
     def along(self, row, way, own=False):
         slot = self.slot(2 * row + self.axis.par)
@@ -497,6 +500,7 @@
 
 WEIGHTS = ("w_query", "w_keyvalue", "w_up", "w_down", "w_out")
 INPUTS = ("tokens", "cotangent") + WEIGHTS
+OUTPUTS = ("mixed_sum", "scaled_sum", "s_w_query", "s_w_out", "s_w_up", "s_w_down", "shared_kv", "shared_norms")
 
 
 def own_shapes(z):
@@ -507,19 +511,27 @@
         queries=((z.rows // BLOCK, z.stack, 128), BF16), keys=((z.rows, 128), BF16), values=((z.rows, 128), BF16),
         scores=((z.used // BLOCK * z.stack, BLOCK), F32), attended=((z.rows, z.wide), BF16), hidden=((z.rows, z.units), BF16),
         slope=((z.rows, z.units), BF16), d_attended=((z.used // BLOCK, z.stack, 128), BF16),
-        d_query=((z.used, z.wide), BF16), d_keyvalue=((z.used, 128), BF16), d_norms=((4, 8, z.model), F32),
+        d_keyvalue=((z.used, 128), BF16), d_norms=((4, 8, z.model), F32),
     )
 
 
 class Names:
     def __init__(self, names, refs):
         self.__dict__.update(zip(names, refs, strict=True))
+
+
+def output_shapes(z):
+    return [
+        (z.slots, z.model), (z.slots, z.model), (z.own, z.wide), (z.own, z.wide), (z.own, z.units), (z.own, z.units),
+        (z.nt, z.own, 128), (z.nt, 8, z.own),
+    ]
 
 
 def fused_specs(z):
     half, model = z.nd // 2, z.model
     columns = dict(zip(WEIGHTS, (z.wide, 128, z.units, z.units, z.wide)))
     arrays = own_shapes(z)
+    arrays.update({name: (shape, F32) for name, shape in zip(OUTPUTS, output_shapes(z))})
     arrays.update(pack_query=((z.own, z.wide), BF16), pack_out=((z.own, z.wide), BF16))
     arrays.update(tokens=((z.rows, model), BF16), cotangent=((z.rows, model), BF16))
     arrays.update({name: ((model, columns[name]), BF16) for name in WEIGHTS})
@@ -532,22 +544,21 @@
         arrays["last_" + name] = ((max(half - 1, 1) * z.own, columns[name]), BF16)
     arrays.update(g_norms=((z.nd * 8, z.own), F32), held_norms=((half * 8, z.own), F32))
     arrays.update(last_norms=((max(half - 1, 1) * 8, z.own), F32))
-    semaphores = dict(send_mixed=z.nt, recv_mixed=z.nt, send_norms=z.nd, recv_norms=z.nd)
+    semaphores = dict(send_mixed=(z.nt,), recv_mixed=(z.nt,), send_norms=(z.nd,), recv_norms=(z.nd,))
     for name in INPUTS:
         count = z.nd if name in WEIGHTS else z.nt
-        semaphores.update({"send_" + name: count // 2 * 3, "recv_" + name: count})
+        shape = (2, count) if name == "tokens" else (count,)
+        semaphores.update({"send_" + name: shape[:-1] + (count // 2 * 3,), "recv_" + name: shape})
     for name in WEIGHTS:
-        semaphores.update({"out_" + name: z.nd, "in_" + name: z.nd})
-    semaphores.update(pair_send=4, pair_recv=4, line_send=2, line_recv=2, local=len(INPUTS))
-    semaphores.update(share_send=2 * z.nt, share_recv=2 * z.nt)
+        semaphores.update({"out_" + name: (z.nd,), "in_" + name: (z.nd,)})
+    semaphores.update(pair_send=(4,), pair_recv=(4,), line_send=(2,), line_recv=(2,), local=(len(INPUTS) + 1,))
+    semaphores.update(share_send=(2 * z.nt,), share_recv=(2 * z.nt,), store=(len(OUTPUTS),))
     return arrays, semaphores
 
 
-OUTPUTS = ("mixed_sum", "scaled_sum", "s_w_query", "s_w_out", "s_w_up", "s_w_down", "shared_kv", "shared_norms")
-
-
 def fused_kernel(z, names, *refs):
-    it = Names(("seq", "norms") + tuple("i_" + n for n in INPUTS) + OUTPUTS + names, refs)
+    vectors, refs = refs[1:5], refs[:1] + refs[5:]
+    it = Names(("seq",) + tuple("i_" + n for n in INPUTS) + tuple("o_" + n for n in OUTPUTS) + names, refs)
     dp, tensor = Axis("dp", z.nd), Axis("tensor", z.nt)
     rows, model, used, slots = z.rows, z.model, z.used, z.slots
     core = Core(z.heads, it.seq[0, 0], **{n: getattr(it, n) for n in tuple(own_shapes(z)) + INPUTS}, grad=it.cotangent, scaled=it.tokens)
@@ -560,16 +571,24 @@
     first = width // 128 * 128
     tail = jnp.concatenate([it.i_w_query[:, first:].astype(F32), pad.astype(F32)], axis=1)
     it.pack_query[:, :first] = it.i_w_query[:, :first]
-    it.pack_query[:, first:] = jnp.where(lane < width - first, tail, it.norms[...].astype(F32)).astype(BF16)
+    start = width - first
+    turned = [v[...].astype(F32).reshape(1, z.own) for v in vectors]
+    turned = jnp.concatenate([jnp.zeros((start, z.own), F32)] + turned + [jnp.zeros((124 - start, z.own), F32)])
+    turned = jnp.concatenate([turned, jnp.zeros((128, 128 - z.own), F32)], axis=1).T[: z.own]
+    it.pack_query[:, first:] = jnp.where(lane < start, tail, turned).astype(BF16)
     it.pack_out[:, :first] = it.i_w_out[:, :first]
     it.pack_out[:, first:] = jnp.concatenate([it.i_w_out[:, first:], pad], axis=1)
     sources = dict(w_query=it.pack_query, w_out=it.pack_out)
     g = {}
     for i, name in enumerate(INPUTS):
-        axis = tensor if name in ("tokens", "cotangent") else dp
+        axis = dp if name in WEIGHTS else tensor
         source = sources.get(name, getattr(it, "i_" + name))
-        sems = getattr(it, "send_" + name), getattr(it, "recv_" + name)
-        g[name] = Gather(axis, source, getattr(it, name), *sems, it.local.at[i])
+        send, recv = getattr(it, "send_" + name), getattr(it, "recv_" + name)
+        g[name] = Gather(axis, source, getattr(it, name), send, recv, it.local.at[i])
+    tokens = [
+        Gather(tensor, it.i_tokens, it.tokens, it.send_tokens.at[h], it.recv_tokens.at[h], it.local.at[len(INPUTS) * h], h, 2)
+        for h in range(2)
+    ]
     pl.semaphore_wait(barrier, expected)
 
     def hand_on(names, distance):
@@ -577,21 +596,20 @@
             g[name].pass_on(distance)
 
     small = ("w_query", "w_keyvalue")
-    for name in ("tokens", "cotangent"):
-        g[name].start_line()
-        g[name].start_pair()
+    for gather in tokens + [g["cotangent"]]:
+        gather.start_line()
+        gather.start_pair()
     for name in small:
         g[name].start_line()
         g[name].start_pair()
     g["w_up"].start_pair()
-    for name in INPUTS:
-        g[name].copy.start()
+    for gather in tokens + [g[name] for name in INPUTS[1:]]:
+        gather.copy.start()
     core.tables(0)
     hand_on(small, 1)
     g["w_up"].start_line()
     core.tables(1)
     hand_on(small, 2)
-    g["w_down"].start_pair()
     hand_on(small, 3)
     hand_on(("w_up",), 1)
     g["w_down"].start_line()
@@ -599,50 +617,59 @@
         g[name].arrive()
     core.unpack_params()
 
-    def enter(slot):
-        for part in range(slots // BLOCK):
-            core.normalize(slot * (slots // BLOCK) + part)
-            core.project(slot * (slots // BLOCK) + part)
-
-    g["tokens"].copy.wait()
+    for gather in tokens:
+        gather.copy.wait()
+    other, other_pair = tensor.line(1), tensor.line(1) + tensor.pair - tensor.me
 
     @pl.loop(0, 4)
     def _(index):
         @pl.when(index == 1)
         def _():
-            g["tokens"].pair_arrived(tensor.row)
+            for gather in tokens:
+                gather.pair_arrived(tensor.row)
             hand_on(("w_up",), 2)
+            g["w_down"].start_pair()
+            g["w_out"].start_line()
+
+        for half in range(2):
+
+            @pl.when(index == 2 + half)
+            def _():
+                tokens[half].pass_on(1)
+                if half == 0:
+                    hand_on(("w_up",), 3)
+                tokens[half].pair_arrived(1 - tensor.row)
+                tokens[half].leave()
+
+        late = index // 2
+        first = jnp.where(index == 0, 2 * tensor.me, 2 * tensor.pair)
+        blocks = [
+            (1 - late) * first + late * (2 * other + index - 2),
+            (1 - late) * (first + 1) + late * (2 * other_pair + index - 2),
+        ]
+        for block in blocks:
+            core.normalize(block)
+            core.project(block)
+
+        @pl.when(index == 2)
+        def _():
+            hand_on(("w_down",), 1)
             g["w_out"].start_pair()
 
-        @pl.when(index == 2)
-        def _():
-            hand_on(("w_up",), 3)
-            hand_on(("w_down",), 1)
-            g["w_out"].start_line()
-            g["tokens"].pass_on(1)
-            g["tokens"].leave()
-
-        @pl.when(index == 3)
-        def _():
-            g["tokens"].pair_arrived(1 - tensor.row)
-            hand_on(("w_down",), 2)
-
-        enter(tensor.me + lax.rem(index, 2) * (tensor.pair - tensor.me) + index // 2 * (tensor.line(1) - tensor.me))
+    hand_on(("w_down",), 2)
+    g["w_up"].arrive()
+
+    @pl.loop(0, rows // slots)
+    def _(index):
+        core.feed(pl.ds(pl.multiple_of(index * slots, slots), slots))
+        for step, (name, distance) in enumerate((("w_down", 3), ("w_out", 1), ("w_out", 2), ("w_out", 3))):
+
+            @pl.when(index == step)
+            def _():
+                hand_on((name,), distance)
 
     for block in range(rows // BLOCK):
         core.attend(block)
-        if block == 3:
-            hand_on(("w_down",), 3)
-            hand_on(("w_out",), 1)
-        if block == 5:
-            hand_on(("w_out",), 2)
-    hand_on(("w_out",), 3)
-    g["w_up"].arrive()
-
-    @pl.loop(0, rows // slots)
-    def _(index):
-        core.feed(pl.ds(pl.multiple_of(index * slots, slots), slots))
-
     g["cotangent"].pass_on(1)
     g["w_down"].arrive()
     g["cotangent"].arrive()
@@ -713,13 +740,14 @@
     def _(index):
         block = chunks - 1 - index
         core.attend_back(block)
+
+        @pl.when(index > 0)
+        def _():
+            scaled.take(block + 1)
+
         part_of(it.mixed, block, BLOCK)[...] = core.input_grad(block).astype(BF16)
         scaled.give(block)
 
-        @pl.when(index > 0)
-        def _():
-            scaled.take(block + 1)
-
         @pl.when(index == 1)
         def _():
             r["w_out"].middle()
@@ -728,8 +756,6 @@
         def _():
             r["w_up"].middle()
 
-    weight_grad("w_query", core.normed1, core.d_query)
-    r["w_query"].start()
     weight_grad("w_keyvalue", core.normed1, core.d_keyvalue)
     r["w_keyvalue"].start()
     part = model // dp.size
@@ -737,9 +763,26 @@
     for i in range(dp.size):
         it.g_norms[i * 8 : (i + 1) * 8] = sums[:, i * part : (i + 1) * part]
     r["norms"].start()
+    weight_grad("w_query", core.normed1, core.d_query)
+    r["w_query"].start()
+    stores = []
+
+    def store(*some):
+        for name in some:
+            index = OUTPUTS.index(name)
+            stores.append(pltpu.make_async_copy(getattr(it, name), getattr(it, "o_" + name), it.store.at[index]))
+            stores[-1].start()
+
     scaled.take(0)
-    for name in ("w_query", "w_keyvalue", "norms"):
+    r["mixed"].end()
+    store("mixed_sum")
+    for name in ("w_keyvalue", "norms"):
         r[name].middle()
+    r["w_down"].end()
+    r["w_query"].middle()
+    r["w_out"].end()
+    r["w_up"].end()
+    store("s_w_down", "s_w_out", "s_w_up")
     for name in ("w_keyvalue", "norms"):
         r[name].end()
     copies = []
@@ -749,49 +792,48 @@
             sems = [s.at[i * tensor.size + step] for s in (it.share_send, it.share_recv)]
             copies.append(remote(ref.at[tensor.me], ref.at[tensor.me], *sems, tensor, peer))
             copies[-1].start()
-    for name in ("w_down", "w_out", "w_up", "mixed", "w_query"):
-        r[name].end()
+    r["w_query"].end()
+    store("s_w_query")
+
     @pl.loop(0, chunks)
     def _(index):
         scaled.end(chunks - 1 - index)
 
+    store("scaled_sum")
     for copy in copies:
         copy.wait()
-    for name in INPUTS:
-        if name in WEIGHTS:
-            g[name].leave()
-
-
-def finish_kernel(heads, seq, tokens, cotangent, *refs):
+    store("shared_kv", "shared_norms")
+    for name in WEIGHTS:
+        g[name].leave()
+    for copy in stores:
+        copy.wait()
+
+
+def finish_kernel(z, seq, tokens, cotangent, *refs):
     sums = Names(OUTPUTS, refs[: len(OUTPUTS)])
-    out_tokens, d_tokens, d_query, d_keyvalue, d_out, d_up, d_down, d_norms = refs[len(OUTPUTS) :]
-    rows, chunk = tokens.shape[0], 128
-    first_row = lax.axis_index("tensor") * rows
-
-    @pl.loop(0, rows // chunk)
-    def _(index):
-        first = pl.multiple_of(index * chunk, chunk)
-        at = pl.ds(first, chunk)
-        token = tokens[at].astype(F32)
-        out_tokens[at] = (token + sums.mixed_sum[at]).astype(BF16)
-        centered = token - jnp.mean(token, axis=1, keepdims=True)
-        inv_std = lax.rsqrt(jnp.mean(centered * centered, axis=1, keepdims=True) + EPS)
-        scaled = centered * inv_std
-        grad = sums.scaled_sum[at]
-        row = lax.broadcasted_iota(jnp.int32, (chunk, 1), 0) + first + first_row
-        own = jnp.where(row < seq[0, 0], cotangent[at].astype(F32), 0.0)
-        inner = jnp.mean(grad * scaled, axis=1, keepdims=True)
-        d_tokens[at] = own + inv_std * (grad - jnp.mean(grad, axis=1, keepdims=True) - scaled * inner)
-
-    d_query[...] = sums.s_w_query[:, : heads * 64]
-    d_out[...] = sums.s_w_out[:, : heads * 64]
+    out_tokens, d_tokens, d_query, d_keyvalue, d_out, d_up, d_down, *d_norms = refs[len(OUTPUTS) :]
+    rows = tokens.shape[0]
+    token = tokens[...].astype(F32)
+    out_tokens[...] = (token + sums.mixed_sum[...]).astype(BF16)
+    centered = token - jnp.mean(token, axis=1, keepdims=True)
+    inv_std = lax.rsqrt(jnp.mean(centered * centered, axis=1, keepdims=True) + EPS)
+    scaled = centered * inv_std
+    grad = sums.scaled_sum[...]
+    first_row = lax.axis_index("tensor") * z.slots + pl.program_id(0) * rows
+    row = lax.broadcasted_iota(jnp.int32, (rows, 1), 0) + first_row
+    own = jnp.where(row < seq[0, 0], cotangent[...].astype(F32), 0.0)
+    inner = jnp.mean(grad * scaled, axis=1, keepdims=True)
+    d_tokens[...] = own + inv_std * (grad - jnp.mean(grad, axis=1, keepdims=True) - scaled * inner)
+    d_query[...] = sums.s_w_query[:, : z.heads * 64]
+    d_out[...] = sums.s_w_out[:, : z.heads * 64]
     d_up[...] = sums.s_w_up[...]
     d_down[...] = sums.s_w_down[...]
     kv, norms = sums.shared_kv[0], sums.shared_norms[0]
-    for t in range(1, sums.shared_kv.shape[0]):
+    for t in range(1, z.nt):
         kv, norms = kv + sums.shared_kv[t], norms + sums.shared_norms[t]
     d_keyvalue[...] = kv
-    d_norms[...] = norms
+    for i in range(4):
+        d_norms[i][...] = norms[i]
 
 
 def plain_kernel(z, seq, *refs):
@@ -863,8 +905,9 @@
     width, model = w_query.shape[1], tokens.shape[1]
     wide = z.wide
     pad = jnp.pad(w_query[:, width // 128 * 128 :], ((0, 0), (0, wide - width)))
-    lane = lax.iota(jnp.int32, 128)[None]
-    tail = jnp.where(lane < width % 128, pad, norms)
+    lane, start = lax.iota(jnp.int32, 128)[None], width % 128
+    vectors = jnp.pad(jnp.stack(norms, axis=1), ((0, 0), (start, 124 - start)))
+    tail = jnp.where(lane < start, pad, vectors)
     query = jnp.concatenate([w_query[:, : width // 128 * 128], tail], axis=1)
     out = jnp.pad(w_out, ((0, 0), (0, wide - width)))
     gathered = [lax.all_gather(a, "tensor", axis=0, tiled=True) for a in (tokens, cotangent)]
@@ -893,21 +936,19 @@
 
 def run_whole(seq_lengths, norms, arrays, z):
     arrays_of, semaphores = fused_specs(z)
-    shapes = [
-        (z.slots, z.model), (z.slots, z.model), (z.own, z.wide), (z.own, z.wide), (z.own, z.units), (z.own, z.units),
-        (z.nt, z.own, 128), (z.nt, 8, z.own),
-    ]
     scratch = [pltpu.VMEM(*entry) for entry in arrays_of.values()]
-    scratch += [pltpu.SemaphoreType.DMA((count,)) for count in semaphores.values()]
+    scratch += [pltpu.SemaphoreType.DMA(shape) for shape in semaphores.values()]
     return pl.pallas_call(
         functools.partial(fused_kernel, z, tuple(arrays_of) + tuple(semaphores)),
-        out_shape=[jax.ShapeDtypeStruct(shape, F32) for shape in shapes],
-        in_specs=[pl.BlockSpec(memory_space=pltpu.SMEM)] + [INVMEM] * (1 + len(arrays)),
-        out_specs=[INVMEM] * len(shapes),
+        out_shape=[jax.ShapeDtypeStruct(shape, F32) for shape in output_shapes(z)],
+        in_specs=[pl.BlockSpec(memory_space=pltpu.SMEM)]
+        + [INVMEM] * 4
+        + [INVMEM if packed else ANY for packed in (False, False, True, False, False, False, True)],
+        out_specs=[ANY] * len(OUTPUTS),
         scratch_shapes=scratch,
         compiler_params=pltpu.CompilerParams(collective_id=0, has_side_effects=True, vmem_limit_bytes=67043328),
         name="layer",
-    )(seq_lengths, norms, *arrays)
+    )(seq_lengths, *norms, *arrays)
 
 
 def run_layer(seq_lengths, norms, arrays, nd, nt):
@@ -920,19 +961,33 @@
     )
     run = run_whole if own % 32 == 0 and slots == 2 * BLOCK and nt == 4 else run_plain
     sums = run(seq_lengths, norms, arrays, z)
+    steps = 2 if own % 16 == 0 else 1
     shape = jax.ShapeDtypeStruct
+
+    def block(rows, columns):
+        return pl.BlockSpec((rows // steps, columns), lambda i: (i, 0))
+
+    width = heads * 64
+    token_rows = block(slots, model)
+    weights = [block(own, n) for n in (z.wide, z.wide, units, units)]
+    shared = [
+        pl.BlockSpec((nt, own // steps, 128), lambda i: (0, i, 0)),
+        pl.BlockSpec((nt, 8, own), lambda i: (0, 0, 0)),
+    ]
     results = pl.pallas_call(
-        functools.partial(finish_kernel, heads),
-        out_shape=[
-            shape((slots, model), BF16), shape((slots, model), F32), shape((own, heads * 64), F32), shape((own, 128), F32),
-            shape((own, heads * 64), F32), shape((own, units), F32), shape((own, units), F32), shape((8, own), F32),
-        ],
-        in_specs=[pl.BlockSpec(memory_space=pltpu.SMEM)] + [INVMEM] * (2 + len(sums)),
-        out_specs=[INVMEM] * 8,
+        functools.partial(finish_kernel, z),
+        grid=(steps,),
+        out_shape=[shape((slots, model), BF16), shape((slots, model), F32)]
+        + [shape((own, n), F32) for n in (width, 128, width, units, units)]
+        + [shape((own,), F32)] * 4,
+        in_specs=[pl.BlockSpec(memory_space=pltpu.SMEM)] + [token_rows] * 4 + weights + shared,
+        out_specs=[token_rows] * 2
+        + [block(own, n) for n in (width, 128, width, units, units)]
+        + [pl.BlockSpec((own,), lambda i: (0,))] * 4,
         compiler_params=pltpu.CompilerParams(vmem_limit_bytes=67043328),
         name="finish",
     )(seq_lengths, *arrays[:2], *sums)
-    return tuple(results[:7]) + tuple(results[7][i] for i in range(4))
+    return tuple(results)
 
 
 def shards(
@@ -949,9 +1004,7 @@
     norm2_gain,
     norm2_bias,
 ):
-    start = w_query.shape[1] % 128
-    norms = jnp.stack([norm1_gain, norm1_bias, norm2_gain, norm2_bias], axis=1)
-    norms = jnp.pad(norms, ((0, 0), (start, 124 - start)))
+    norms = (norm1_gain, norm1_bias, norm2_gain, norm2_bias)
     arrays = (tokens, cotangent, w_query, w_keyvalue, w_up, w_down, w_out)
     return run_layer(seq_lengths, norms, arrays, lax.axis_size("dp"), lax.axis_size("tensor"))
 

time: 129 us -> 124 us (0.961)
  Pallas kernels: 126 us -> 122 us
  local copies, waits for them, and re-layouts: 2.18 us -> 0 us
    pallas_call x1, Pallas kernels: 120 us -> 118 us  [run_whole(): pl.pallas_call(functools.partial(fused_kernel, z, tuple(arrays_of) + tupl...]
    pallas_call x1, Pallas kernels: 5.63 us -> 4.27 us  [run_layer(): pl.pallas_call(functools.partial(finish_kernel, z), grid=(steps,), out_sh...]
    squeeze x1 -> x0, local copies, waits for them, and re-layouts: 1.36 us -> none  [run_layer(): return tuple(results[:7]) + tuple((results[7][i] for i in range(4)))]
where the time goes in v1:
time: 124 us; the launch traced here: 123 us
  Pallas kernels  122 us (98%)
    pallas_call x1, Pallas kernels, run_whole(): pl.pallas_call(functools.partial(fused_kernel, z, tuple(arrays_of) + tupl...  118 us
    pallas_call x1, Pallas kernels, run_layer(): pl.pallas_call(functools.partial(finish_kernel, z), grid=(steps,), out_sh...  4.27 us

profile of v1, /device:TPU:0, one launch (start us, length us, event | category | flops | bytes accessed | tf_op | source)
XLA Modules:
  0.0 123.3 jit_solution(16979360554457344803)
XLA Ops:
  0.6 118.2 %layer.1 = (f32[512,768]{1,0:T(8,128)}, f32[512,768]{1,0:T(8,128)}, f32[96,256]{1,0:T(8,128)}, f32[96,256]{1,0:T(8,128)}, f32[96,768]{1,0:T(8,128)}, /*index=5*/...) custom-call(s32[1,2]{1,0:T(1,128)} %seq.1, bf16[96]{0:T(256)(128)(2,1)} %refs_1_.1, bf16[96]{0:T(256)(128)(2,1)} %refs_2_.1, ...), custom_call_target="tpu_custom_call" | custom-call | tf_op jit(solution)/shard_map/layer/pallas_call | solution.py:941
  118.9 4.3 %finish.1 = (bf16[512,768]{1,0:T(8,128)(2,1)}, f32[512,768]{1,0:T(8,128)}, f32[96,192]{1,0:T(8,128)}, f32[96,128]{1,0:T(8,128)}, f32[96,192]{1,0:T(8,128)}, /*in...) custom-call(s32[1,2]{1,0:T(1,128)} %seq.1, ...), custom_call_target="tpu_custom_call" | custom-call | tf_op jit(solution)/shard_map/finish/pallas_call | solution.py:977

commit v2 on v1

--- a/solution.py
+++ b/solution.py
@@ -13,6 +13,7 @@
 SEQ_LEAST = 1024
 SEQ_MOST = 1792
 BLOCK = 256
+WIDE = 3
 EPS = 1e-05
 NEG = -1e30
 F32 = jnp.float32
@@ -62,10 +63,10 @@
 
 
 class Core:
-    def __init__(self, heads, length, **refs):
-        self.heads, self.length = heads, length
+    def __init__(self, heads, length, used, **refs):
+        self.heads, self.length, self.used = heads, length, used
         self.__dict__.update(refs)
-        stack, used = heads * BLOCK, self.d_keyvalue.shape[0]
+        stack = heads * BLOCK
         self.d_query = self.attended
         self.d_stack = self.scores.at[0:stack, 0:128]
         self.d_keys = self.scores.at[stack : stack + used, 0:128]
@@ -173,6 +174,12 @@
         d_hidden = dot(self.grad[at], self.w_down[...])
         self.slope[at] = (d_hidden * self.slope[at].astype(F32)).astype(BF16)
 
+    def d_attended(self, block, first, size):
+        across = self.hidden.shape[1] // 128
+        row = block // across * (self.heads * BLOCK) + first
+        lane = lax.rem(block, across) * 128
+        return self.hidden.at[pl.ds(pl.multiple_of(row, BLOCK), size), pl.ds(pl.multiple_of(lane, 128), 128)]
+
     def attend_grad(self, block):
         first = pl.multiple_of(block * BLOCK, BLOCK)
         at = pl.ds(first, BLOCK)
@@ -184,11 +191,11 @@
             delta = jnp.sum(jnp.where(lane < 64, grad * outputs[h], 0.0), axis=1, keepdims=True)
             high, middle, low = three_parts(-delta)
             parts = jnp.where(lane == 64, high, jnp.where(lane == 65, middle, jnp.where(lane == 66, low, 0.0)))
-            self.d_attended[block, h * BLOCK : (h + 1) * BLOCK] = jnp.where(lane < 64, grad, parts).astype(BF16)
+            self.d_attended(block, h * BLOCK, BLOCK)[...] = jnp.where(lane < 64, grad, parts).astype(BF16)
 
     def attend_back(self, block):
         rows = self.heads * BLOCK
-        query, grad = self.queries[block], self.d_attended[block]
+        query, grad = self.queries[block], self.d_attended(block, 0, rows)[...]
 
         def span(first, size, diagonal):
             at = pl.ds(pl.multiple_of(first, BLOCK), size)
@@ -208,36 +215,50 @@
             else:
                 self.d_stack[...] += d_query
 
-        @pl.when(block % 2 == 1)
-        def _():
-            span((block - 1) * BLOCK, 2 * BLOCK, True)
-
-        @pl.when(block % 2 == 0)
-        def _():
-            span(block * BLOCK, BLOCK, True)
-
-        @pl.loop(0, block // 2)
+        last = lax.rem(block, WIDE)
+        for size in range(WIDE):
+
+            @pl.when(last == size)
+            def _():
+                span((block - size) * BLOCK, (size + 1) * BLOCK, True)
+
+        @pl.loop(0, block // WIDE)
         def _(index):
-            span(index * 2 * BLOCK, 2 * BLOCK, False)
+            span(index * WIDE * BLOCK, WIDE * BLOCK, False)
 
         at = pl.ds(pl.multiple_of(block * BLOCK, BLOCK), BLOCK)
-        lane = lanes_of(BLOCK)
-        cosine, sine = self.cosine[at], self.sine[at]
-
-        def turn_back(x):
-            return x * cosine - swap_halves(x, lane) * sine
-
         pieces = [
-            turn_back(self.d_stack[h * BLOCK : (h + 1) * BLOCK]) * (64 ** (-0.5)) for h in range(self.heads)
+            self.turn_back(self.d_stack[h * BLOCK : (h + 1) * BLOCK], at) * (64 ** (-0.5)) for h in range(self.heads)
         ]
-        self.d_query[at] = join_heads(pieces, lane).astype(BF16)
-        self.d_keyvalue[at] = jnp.where(
-            lane < 64, turn_back(self.d_keys[at]), pltpu.roll(self.d_values[at], 64, 1)
-        ).astype(BF16)
+        self.d_query[at] = join_heads(pieces, lanes_of(BLOCK)).astype(BF16)
+
+    def turn_back(self, x, at):
+        return x * self.cosine[at] - swap_halves(x, lanes_of(BLOCK)) * self.sine[at]
+
+    def keyvalue_grad(self):
+        rows = self.d_keyvalue.shape[0]
+
+        @pl.loop(0, self.used // BLOCK)
+        def _(block):
+            at = pl.ds(pl.multiple_of(block * BLOCK, BLOCK), BLOCK)
+            d_keys = self.turn_back(self.d_keys[at], at)
+            d_values = pltpu.roll(self.d_values[at], 64, 1)
+            self.d_keyvalue[at] = jnp.where(lanes_of(BLOCK) < 64, d_keys, d_values).astype(BF16)
+
+        self.d_keyvalue[self.used :] = jnp.zeros((rows - self.used, 128), BF16)
+
+    def keyvalue_norms(self):
+        weight = self.w_keyvalue[...].astype(F32)
+        grad = self.d_keyvalue[: self.used]
+        gain = jnp.sum(dot_rows(self.scaled[: self.used], grad) * weight, axis=1, keepdims=True)
+        bias = jnp.sum(jnp.sum(grad.astype(F32), axis=0, keepdims=True) * weight, axis=1, keepdims=True)
+        lane = lanes_of(weight.shape[0])
+        turned = jnp.where(lane == 0, gain, bias).T
+        return turned[0:1], turned[1:2]
 
     def input_grad(self, block):
         at = pl.ds(pl.multiple_of(block * BLOCK, BLOCK), BLOCK)
-        d_normed1 = dot_cols(self.d_query[at], self.w_query[...]) + dot_cols(self.d_keyvalue[at], self.w_keyvalue[...])
+        d_normed1 = dot_cols(self.d_query[at], self.w_query[...])
         d_normed2 = dot_cols(self.slope[at], self.w_up[...])
         scaled = self.scaled[at].astype(F32)
         for i, value in enumerate((d_normed1 * scaled, d_normed1, d_normed2 * scaled, d_normed2)):
@@ -510,8 +531,7 @@
         normed1=(wide_rows, BF16), normed2=(wide_rows, BF16),
         queries=((z.rows // BLOCK, z.stack, 128), BF16), keys=((z.rows, 128), BF16), values=((z.rows, 128), BF16),
         scores=((z.used // BLOCK * z.stack, BLOCK), F32), attended=((z.rows, z.wide), BF16), hidden=((z.rows, z.units), BF16),
-        slope=((z.rows, z.units), BF16), d_attended=((z.used // BLOCK, z.stack, 128), BF16),
-        d_keyvalue=((z.used, 128), BF16), d_norms=((4, 8, z.model), F32),
+        slope=((z.rows, z.units), BF16), d_keyvalue=((z.rows, 128), BF16), d_norms=((4, 8, z.model), F32),
     )
 
 
@@ -542,9 +562,10 @@
         arrays["g_" + name] = ((model, columns[name]), BF16)
         arrays["held_" + name] = ((half * z.own, columns[name]), BF16)
         arrays["last_" + name] = ((max(half - 1, 1) * z.own, columns[name]), BF16)
+    arrays.update(held_pack=((z.rows // 2, 128), BF16), last_pack=((z.slots, 128), BF16), pack_sum=((z.slots, 128), F32))
     arrays.update(g_norms=((z.nd * 8, z.own), F32), held_norms=((half * 8, z.own), F32))
     arrays.update(last_norms=((max(half - 1, 1) * 8, z.own), F32))
-    semaphores = dict(send_mixed=(z.nt,), recv_mixed=(z.nt,), send_norms=(z.nd,), recv_norms=(z.nd,))
+    semaphores = dict(send_mixed=(z.nt,), recv_mixed=(z.nt,), send_pack=(z.nt,), recv_pack=(z.nt,), send_norms=(z.nd,), recv_norms=(z.nd,))
     for name in INPUTS:
         count = z.nd if name in WEIGHTS else z.nt
         shape = (2, count) if name == "tokens" else (count,)
@@ -561,7 +582,7 @@
     it = Names(("seq",) + tuple("i_" + n for n in INPUTS) + tuple("o_" + n for n in OUTPUTS) + names, refs)
     dp, tensor = Axis("dp", z.nd), Axis("tensor", z.nt)
     rows, model, used, slots = z.rows, z.model, z.used, z.slots
-    core = Core(z.heads, it.seq[0, 0], **{n: getattr(it, n) for n in tuple(own_shapes(z)) + INPUTS}, grad=it.cotangent, scaled=it.tokens)
+    core = Core(z.heads, it.seq[0, 0], z.used, **{n: getattr(it, n) for n in tuple(own_shapes(z)) + INPUTS}, grad=it.cotangent, scaled=it.tokens)
     barrier = pltpu.get_barrier_semaphore()
     expected = dp.greet(barrier) + tensor.greet(barrier)
 
@@ -691,15 +712,20 @@
         dp, it.g_norms, it.shared_norms.at[tensor.me], it.held_norms, it.last_norms, it.send_norms, it.recv_norms
     )
     r["mixed"] = Reduce(tensor, it.mixed, it.mixed_sum, it.held_mixed, it.last_mixed, it.send_mixed, it.recv_mixed)
+    r["pack"] = Reduce(
+        tensor, core.d_keyvalue, it.pack_sum, it.held_pack, it.last_pack, it.send_pack, it.recv_pack
+    )
     scaled = Stream(
         tensor, it.mixed, it.scaled_sum, it.held_scaled, it.last_scaled,
         it.pair_send, it.pair_recv, it.line_send, it.line_recv,
     )
 
     def weight_grad(name, left, right):
-        @pl.loop(0, model // BLOCK)
+        half = model // 2
+
+        @pl.loop(0, 2)
         def _(index):
-            at = pl.ds(pl.multiple_of(index * BLOCK, BLOCK), BLOCK)
+            at = pl.ds(pl.multiple_of(index * half, 128), half)
             r[name].part[at] = dot_rows(left[:used, at], right[:used]).astype(BF16)
 
     weight_grad("w_down", core.grad, core.hidden)
@@ -736,14 +762,17 @@
         ref[...] = jnp.zeros_like(ref)
     chunks = used // BLOCK
 
+    def turn(index):
+        return jnp.where(lax.rem(index, 2) == 0, chunks // 2, chunks - 1) - index // 2
+
     @pl.loop(0, chunks)
     def _(index):
-        block = chunks - 1 - index
+        block = turn(index)
         core.attend_back(block)
 
         @pl.when(index > 0)
         def _():
-            scaled.take(block + 1)
+            scaled.take(turn(index - 1))
 
         part_of(it.mixed, block, BLOCK)[...] = core.input_grad(block).astype(BF16)
         scaled.give(block)
@@ -756,13 +785,20 @@
         def _():
             r["w_up"].middle()
 
+    core.keyvalue_grad()
+    r["pack"].start()
     weight_grad("w_keyvalue", core.normed1, core.d_keyvalue)
     r["w_keyvalue"].start()
+    scaled.take(turn(chunks - 1))
     part = model // dp.size
-    sums = jnp.concatenate([jnp.sum(core.d_norms[i], axis=0, keepdims=True) for i in range(4)] + [jnp.zeros((4, model), F32)])
+    sums = [jnp.sum(core.d_norms[i], axis=0, keepdims=True) for i in range(4)]
+    for i, more in enumerate(core.keyvalue_norms()):
+        sums[i] = sums[i] + more
+    sums = jnp.concatenate(sums + [jnp.zeros((4, model), F32)])
     for i in range(dp.size):
         it.g_norms[i * 8 : (i + 1) * 8] = sums[:, i * part : (i + 1) * part]
     r["norms"].start()
+    r["pack"].middle()
     weight_grad("w_query", core.normed1, core.d_query)
     r["w_query"].start()
     stores = []
@@ -773,7 +809,6 @@
             stores.append(pltpu.make_async_copy(getattr(it, name), getattr(it, "o_" + name), it.store.at[index]))
             stores[-1].start()
 
-    scaled.take(0)
     r["mixed"].end()
     store("mixed_sum")
     for name in ("w_keyvalue", "norms"):
@@ -797,7 +832,14 @@
 
     @pl.loop(0, chunks)
     def _(index):
-        scaled.end(chunks - 1 - index)
+        scaled.end(turn(index))
+
+    r["pack"].end()
+
+    @pl.loop(0, slots // 128)
+    def _(index):
+        at = pl.ds(pl.multiple_of(index * 128, 128), 128)
+        it.scaled_sum[at] += dot_cols(it.pack_sum[at].astype(BF16), core.w_keyvalue[...]) * core.params[0:1]
 
     store("scaled_sum")
     for copy in copies:
@@ -841,7 +883,7 @@
     mixed, scaled_grad, g_query, g_keyvalue, g_out, g_up, g_down, g_norms = refs[len(INPUTS) : len(INPUTS) + 8]
     *own, grad, scaled = refs[len(INPUTS) + 8 :]
     named.update(zip(own_shapes(z), own), grad=grad, scaled=scaled)
-    core = Core(z.heads, seq[0, 0], **named)
+    core = Core(z.heads, seq[0, 0], z.used, **named)
     rows, model, used = z.rows, z.model, z.used
     core.tables(0)
     core.tables(1)
@@ -866,10 +908,6 @@
         first = pl.multiple_of(index * (used // 4), used // 4)
         core.mask(pl.ds(first, used // 4), first, used // 4)
         core.feed_back(pl.ds(first, used // 4))
-
-    @pl.loop(0, used // BLOCK)
-    def _(block):
-        core.attend_grad(block)
 
     @pl.loop(0, model // BLOCK)
     def _(index):
@@ -879,6 +917,10 @@
         g_out[at] = dot_rows(grad, core.attended[:used]).astype(BF16)
         g_up[at] = dot_rows(core.normed2[:used, at], core.slope[:used]).astype(BF16)
 
+    @pl.loop(0, used // BLOCK)
+    def _(block):
+        core.attend_grad(block)
+
     for ref in (core.d_keys, core.d_values, core.d_norms):
         ref[...] = jnp.zeros_like(ref)
     @pl.loop(0, used // BLOCK)
@@ -886,6 +928,14 @@
         block = used // BLOCK - 1 - index
         core.attend_back(block)
         part_of(scaled_grad, block, BLOCK)[...] = core.input_grad(block).astype(BF16)
+
+    core.keyvalue_grad()
+
+    @pl.loop(0, used // BLOCK)
+    def _(block):
+        at = pl.ds(pl.multiple_of(block * BLOCK, BLOCK), BLOCK)
+        more = dot_cols(core.d_keyvalue[at], core.w_keyvalue[...]) * core.params[0:1]
+        scaled_grad[at] = (scaled_grad[at].astype(F32) + more).astype(BF16)
 
     scaled_grad[used:] = jnp.zeros((rows - used, model), BF16)
 
@@ -898,6 +948,8 @@
 
     for i in range(4):
         g_norms[i : i + 1] = jnp.sum(core.d_norms[i], axis=0, keepdims=True)
+    for i, more in enumerate(core.keyvalue_norms()):
+        g_norms[i : i + 1] += more
 
 
 def run_plain(seq_lengths, norms, arrays, z):
@@ -959,7 +1011,7 @@
         nd=nd, nt=nt, heads=heads, rows=slots * nt, model=model, stack=heads * BLOCK, units=units, used=SEQ_MOST,
         wide=(heads * 64 + 4 + 127) // 128 * 128, own=own, slots=slots,
     )
-    run = run_whole if own % 32 == 0 and slots == 2 * BLOCK and nt == 4 else run_plain
+    run = run_whole if own % 32 == 0 and slots == 2 * BLOCK and nt == 4 and SEQ_MOST == 7 * BLOCK else run_plain
     sums = run(seq_lengths, norms, arrays, z)
     steps = 2 if own % 16 == 0 else 1
     shape = jax.ShapeDtypeStruct

time: 124 us -> 121 us (0.976)
  Pallas kernels: 122 us -> 120 us
    pallas_call x1, Pallas kernels: 118 us -> 116 us  [run_whole(): pl.pallas_call(functools.partial(fused_kernel, z, tuple(arrays_of) + tupl...]
where the time goes in v2:
time: 121 us
  Pallas kernels  120 us (99%)
    pallas_call x1, Pallas kernels, run_whole(): pl.pallas_call(functools.partial(fused_kernel, z, tuple(arrays_of) + tupl...  116 us
    pallas_call x1, Pallas kernels, run_layer(): pl.pallas_call(functools.partial(finish_kernel, z), grid=(steps,), out_sh...  4.27 us

profile of v2, /device:TPU:0, one launch (start us, length us, event | category | flops | bytes accessed | tf_op | source)
XLA Modules:
  0.0 121.3 jit_solution(13521298983161761420)
XLA Ops:
  0.6 116.2 %layer.1 = (f32[512,768]{1,0:T(8,128)}, f32[512,768]{1,0:T(8,128)}, f32[96,256]{1,0:T(8,128)}, f32[96,256]{1,0:T(8,128)}, f32[96,768]{1,0:T(8,128)}, /*index=5*/...) custom-call(s32[1,2]{1,0:T(1,128)} %seq.1, bf16[96]{0:T(256)(128)(2,1)} %refs_1_.1, bf16[96]{0:T(256)(128)(2,1)} %refs_2_.1, ...), custom_call_target="tpu_custom_call" | custom-call | tf_op jit(solution)/shard_map/layer/pallas_call | solution.py:993
  116.8 4.3 %finish.1 = (bf16[512,768]{1,0:T(8,128)(2,1)}, f32[512,768]{1,0:T(8,128)}, f32[96,192]{1,0:T(8,128)}, f32[96,128]{1,0:T(8,128)}, f32[96,192]{1,0:T(8,128)}, /*in...) custom-call(s32[1,2]{1,0:T(1,128)} %seq.1, ...), custom_call_target="tpu_custom_call" | custom-call | tf_op jit(solution)/shard_map/finish/pallas_call | solution.py:1029

commit v3 on v2

--- a/solution.py
+++ b/solution.py
@@ -284,11 +284,10 @@
     def line(self, step):
         return self.other_row(step) * 2 + self.par
 
-    def greet(self, barrier):
-        for step in range(1, self.size):
-            peer = lax.rem(self.me + step, self.size)
+    def greet(self, barrier, peers):
+        for peer in peers:
             pl.semaphore_signal(barrier, inc=1, device_id={self.name: peer}, device_id_type=MESH)
-        return self.size - 1
+        return len(peers)
 
 
 def remote(src, dst, send, recv, axis, peer):
@@ -584,7 +583,8 @@
     rows, model, used, slots = z.rows, z.model, z.used, z.slots
     core = Core(z.heads, it.seq[0, 0], z.used, **{n: getattr(it, n) for n in tuple(own_shapes(z)) + INPUTS}, grad=it.cotangent, scaled=it.tokens)
     barrier = pltpu.get_barrier_semaphore()
-    expected = dp.greet(barrier) + tensor.greet(barrier)
+    expected = dp.greet(barrier, [dp.pair] + [dp.line(step) for step in range(1, dp.half)])
+    expected += tensor.greet(barrier, [lax.rem(tensor.me + step, tensor.size) for step in range(1, tensor.size)])
 
     width = z.heads * 64
     pad = jnp.zeros((z.own, z.wide - width), BF16)
@@ -786,10 +786,10 @@
             r["w_up"].middle()
 
     core.keyvalue_grad()
+    scaled.take(turn(chunks - 1))
     r["pack"].start()
     weight_grad("w_keyvalue", core.normed1, core.d_keyvalue)
     r["w_keyvalue"].start()
-    scaled.take(turn(chunks - 1))
     part = model // dp.size
     sums = [jnp.sum(core.d_norms[i], axis=0, keepdims=True) for i in range(4)]
     for i, more in enumerate(core.keyvalue_norms()):
@@ -809,15 +809,8 @@
             stores.append(pltpu.make_async_copy(getattr(it, name), getattr(it, "o_" + name), it.store.at[index]))
             stores[-1].start()
 
-    r["mixed"].end()
-    store("mixed_sum")
-    for name in ("w_keyvalue", "norms"):
+    for name in ("w_keyvalue", "norms", "w_query"):
         r[name].middle()
-    r["w_down"].end()
-    r["w_query"].middle()
-    r["w_out"].end()
-    r["w_up"].end()
-    store("s_w_down", "s_w_out", "s_w_up")
     for name in ("w_keyvalue", "norms"):
         r[name].end()
     copies = []
@@ -827,6 +820,12 @@
             sems = [s.at[i * tensor.size + step] for s in (it.share_send, it.share_recv)]
             copies.append(remote(ref.at[tensor.me], ref.at[tensor.me], *sems, tensor, peer))
             copies[-1].start()
+    r["mixed"].end()
+    store("mixed_sum")
+    r["w_down"].end()
+    r["w_out"].end()
+    r["w_up"].end()
+    store("s_w_down", "s_w_out", "s_w_up")
     r["w_query"].end()
     store("s_w_query")
 

time: 121 us -> 121 us (level)
  no operation moved by 1% of the time
where the time goes in v3:
time: 121 us
  Pallas kernels  120 us (99%)
    pallas_call x1, Pallas kernels, run_whole(): pl.pallas_call(functools.partial(fused_kernel, z, tuple(arrays_of) + tupl...  116 us
    pallas_call x1, Pallas kernels, run_layer(): pl.pallas_call(functools.partial(finish_kernel, z), grid=(steps,), out_sh...  4.27 us

profile of v3, /device:TPU:0, one launch (start us, length us, event | category | flops | bytes accessed | tf_op | source)
XLA Modules:
  0.0 120.7 jit_solution(8167374199179393867)
XLA Ops:
  0.6 115.6 %layer.1 = (f32[512,768]{1,0:T(8,128)}, f32[512,768]{1,0:T(8,128)}, f32[96,256]{1,0:T(8,128)}, f32[96,256]{1,0:T(8,128)}, f32[96,768]{1,0:T(8,128)}, /*index=5*/...) custom-call(s32[1,2]{1,0:T(1,128)} %seq.1, bf16[96]{0:T(256)(128)(2,1)} %refs_1_.1, bf16[96]{0:T(256)(128)(2,1)} %refs_2_.1, ...), custom_call_target="tpu_custom_call" | custom-call | tf_op jit(solution)/shard_map/layer/pallas_call | solution.py:992
  116.2 4.3 %finish.1 = (bf16[512,768]{1,0:T(8,128)(2,1)}, f32[512,768]{1,0:T(8,128)}, f32[96,192]{1,0:T(8,128)}, f32[96,128]{1,0:T(8,128)}, f32[96,192]{1,0:T(8,128)}, /*in...) custom-call(s32[1,2]{1,0:T(1,128)} %seq.1, ...), custom_call_target="tpu_custom_call" | custom-call | tf_op jit(solution)/shard_map/finish/pallas_call | solution.py:1028

commit v4 on v3

--- a/solution.py
+++ b/solution.py
@@ -387,7 +387,7 @@
     def __init__(self, axis, part, out, held, last, send, recv):
         self.axis, self.part, self.out, self.held, self.last = axis, part, out, held, last
         self.send, self.recv, self.rows = send, recv, out.shape[0]
-        self.chunk = 32 if self.rows % 32 == 0 else self.rows
+        self.chunk = 64 if self.rows % 64 == 0 else self.rows
 
     def first(self, row):
         block = part_of(self.part, 2 * row + 1 - self.axis.par, self.rows)

time: 121 us -> 120 us (level)
  no operation moved by 1% of the time
where the time goes in v4:
time: 120 us
  Pallas kernels  119 us (99%)
    pallas_call x1, Pallas kernels, run_whole(): pl.pallas_call(functools.partial(fused_kernel, z, tuple(arrays_of) + tupl...  115 us
    pallas_call x1, Pallas kernels, run_layer(): pl.pallas_call(functools.partial(finish_kernel, z), grid=(steps,), out_sh...  4.27 us

profile of v4, /device:TPU:0, one launch (start us, length us, event | category | flops | bytes accessed | tf_op | source)
XLA Modules:
  0.0 120.1 jit_solution(11376023933925217571)
XLA Ops:
  0.6 115.0 %layer.1 = (f32[512,768]{1,0:T(8,128)}, f32[512,768]{1,0:T(8,128)}, f32[96,256]{1,0:T(8,128)}, f32[96,256]{1,0:T(8,128)}, f32[96,768]{1,0:T(8,128)}, /*index=5*/...) custom-call(s32[1,2]{1,0:T(1,128)} %seq.1, bf16[96]{0:T(256)(128)(2,1)} %refs_1_.1, bf16[96]{0:T(256)(128)(2,1)} %refs_2_.1, ...), custom_call_target="tpu_custom_call" | custom-call | tf_op jit(solution)/shard_map/layer/pallas_call | solution.py:992
  115.6 4.3 %finish.1 = (bf16[512,768]{1,0:T(8,128)(2,1)}, f32[512,768]{1,0:T(8,128)}, f32[96,192]{1,0:T(8,128)}, f32[96,128]{1,0:T(8,128)}, f32[96,192]{1,0:T(8,128)}, /*in...) custom-call(s32[1,2]{1,0:T(1,128)} %seq.1, ...), custom_call_target="tpu_custom_call" | custom-call | tf_op jit(solution)/shard_map/finish/pallas_call | solution.py:1028

commit v5 on v4

--- a/solution.py
+++ b/solution.py
@@ -478,22 +478,22 @@
             self.pair_copy(chunk).wait_recv()
 
             def total(at):
-                part = self.part[pl.ds(chunk * BLOCK + at, 32)].astype(F32)
-                return part + self.held[pl.ds((2 * row + half) * BLOCK + at, 32)].astype(F32)
+                part = self.part[pl.ds(chunk * BLOCK + at, 64)].astype(F32)
+                return part + self.held[pl.ds((2 * row + half) * BLOCK + at, 64)].astype(F32)
 
             @pl.when(self.axis.row == row)
             def _():
-                @pl.loop(0, BLOCK // 32)
+                @pl.loop(0, BLOCK // 64)
                 def _(index):
-                    at = pl.multiple_of(index * 32, 32)
-                    self.out[pl.ds(half * BLOCK + at, 32)] = total(at)
+                    at = pl.multiple_of(index * 64, 64)
+                    self.out[pl.ds(half * BLOCK + at, 64)] = total(at)
 
             @pl.when(self.axis.row != row)
             def _():
-                @pl.loop(0, BLOCK // 32)
+                @pl.loop(0, BLOCK // 64)
                 def _(index):
-                    at = pl.multiple_of(index * 32, 32)
-                    self.held[pl.ds((2 * row + half) * BLOCK + at, 32)] = total(at).astype(BF16)
+                    at = pl.multiple_of(index * 64, 64)
+                    self.held[pl.ds((2 * row + half) * BLOCK + at, 64)] = total(at).astype(BF16)
 
                 self.line_copy(chunk).start()
 
@@ -512,10 +512,10 @@
         def _():
             self.line_copy(chunk).wait_recv()
 
-            @pl.loop(0, BLOCK // 32)
+            @pl.loop(0, BLOCK // 64)
             def _(index):
-                at = pl.multiple_of(index * 32, 32)
-                rows = pl.ds(half * BLOCK + at, 32)
+                at = pl.multiple_of(index * 64, 64)
+                rows = pl.ds(half * BLOCK + at, 64)
                 self.out[rows] += self.last[rows].astype(F32)
 
 WEIGHTS = ("w_query", "w_keyvalue", "w_up", "w_down", "w_out")

time: 120 us -> 120 us (level)
  no operation moved by 1% of the time
where the time goes in v5:
time: 120 us
  Pallas kernels  119 us (99%)
    pallas_call x1, Pallas kernels, run_whole(): pl.pallas_call(functools.partial(fused_kernel, z, tuple(arrays_of) + tupl...  115 us
    pallas_call x1, Pallas kernels, run_layer(): pl.pallas_call(functools.partial(finish_kernel, z), grid=(steps,), out_sh...  4.27 us

profile of v5, /device:TPU:0, one launch (start us, length us, event | category | flops | bytes accessed | tf_op | source)
XLA Modules:
  0.0 120.0 jit_solution(17115460173750540485)
XLA Ops:
  0.6 114.8 %layer.1 = (f32[512,768]{1,0:T(8,128)}, f32[512,768]{1,0:T(8,128)}, f32[96,256]{1,0:T(8,128)}, f32[96,256]{1,0:T(8,128)}, f32[96,768]{1,0:T(8,128)}, /*index=5*/...) custom-call(s32[1,2]{1,0:T(1,128)} %seq.1, bf16[96]{0:T(256)(128)(2,1)} %refs_1_.1, bf16[96]{0:T(256)(128)(2,1)} %refs_2_.1, ...), custom_call_target="tpu_custom_call" | custom-call | tf_op jit(solution)/shard_map/layer/pallas_call | solution.py:992
  115.5 4.3 %finish.1 = (bf16[512,768]{1,0:T(8,128)(2,1)}, f32[512,768]{1,0:T(8,128)}, f32[96,192]{1,0:T(8,128)}, f32[96,128]{1,0:T(8,128)}, f32[96,192]{1,0:T(8,128)}, /*in...) custom-call(s32[1,2]{1,0:T(1,128)} %seq.1, ...), custom_call_target="tpu_custom_call" | custom-call | tf_op jit(solution)/shard_map/finish/pallas_call | solution.py:1028
